TPU v7x, 128 devices: a whole 4x4x4 slice. The times are simulated.
128 devices in a mesh: tok: 4 (over y), seq: 16 (over z, x), kv: 2 (over core).
Axes of the slice: x: 4, y: 4, z: 4, core: 2. Of those that a mesh axis runs over, the one named last changes fastest.
Arguments:
- token_ids: int32 [64, 4], replicated, may hold values from 0 to 32767
- request_order: int32 [64], replicated, may hold values from 0 to 63, each once
- cache_lengths: int32 [64], replicated, may hold values from 1 to 16384, 524288 in all
- embed_table: bfloat16 [32768, 2048], P(('tok', 'kv'), 'seq'), may hold values from -3 to 3
- attn_gain: bfloat16 [2048], replicated, may hold values from 0.099609375 to 1.8984375
- proj_query: bfloat16 [2048, 2048], P(None, ('tok', 'kv')), may hold values from -0.125 to 0.125
- proj_kv: bfloat16 [2048, 8, 128], P(None, ('tok', 'kv')), may hold values from -0.125 to 0.125
- kv_cache: bfloat16 [64, 16384, 8, 128], P(None, 'seq', ('tok', 'kv')), may hold values from -125 to 125, as said below
- proj_out: bfloat16 [2048, 2048], P(('tok', 'kv'), 'seq'), may hold values from -0.25 to 0.25
- mlp_gain: bfloat16 [2048], replicated, may hold values from 0.099609375 to 1.8984375
- proj_gate: bfloat16 [2048, 8192], P(None, 'seq'), may hold values from -0.125 to 0.125
- proj_up: bfloat16 [2048, 8192], P(None, 'seq'), may hold values from -0.125 to 0.125
- proj_down: bfloat16 [8192, 2048], P('seq'), may hold values from -0.0625 to 0.0625
Outputs:
- hidden_out: bfloat16 [64, 4, 2048], P(('tok', 'kv'), None, 'seq')
Inputs may be any that keep to these rules, and one draw needn't show every extreme that they name: `request_order`: every request stands in exactly one slot. `cache_lengths`: the lengths sum to 524288 and the largest equals 16384. `kv_cache`: cached keys are already rotated to their positions.
All inputs are finite; a program needn't handle non-finite values.
Results may differ from a plain program's by a relative error of at most 0.018.
The roundings to bfloat16 on the way count: a program that leaves them out, or rounds other values in their place, can miss the bound.
Values may be sent and summed in bfloat16 or wider, within the bound.
A program may use at most 128 MiB of HBM per device.

v0:
```python
import jax
import jax.numpy as jnp
from jax import lax
from jax.sharding import PartitionSpec as P

EPSILON = 1e-05
ROPE_BASE = 1000000.0
FLOOR_SCORE = -1e30


def combined_all(value, axis, join):
    pieces = jax.tree.map(lambda part: lax.all_gather(part, axis), value)
    head = jax.tree.map(lambda part: part[0], pieces)
    tail = jax.tree.map(lambda part: part[1:], pieces)
    so_far, _ = lax.scan(lambda so_far, share: (join(so_far, share), None), head, tail)
    return so_far


def rotate(vector, position):
    half_dim = vector.shape[-1] // 2
    frequency = ROPE_BASE ** (-(jnp.arange(half_dim, dtype=jnp.float32) * 2.0 / vector.shape[-1]))
    angles = position[..., None] * frequency
    cosine = jnp.cos(angles)
    sine_part = jnp.sin(angles)
    front_half = vector[..., :half_dim]
    back_half = vector[..., half_dim:]
    return jnp.concatenate(
        [front_half * cosine - back_half * sine_part, back_half * cosine + front_half * sine_part],
        axis=-1,
    )


def combine(earlier, later):
    peak_a, mass_a, accum_a = earlier
    peak_b, mass_b, accum_b = later
    highest = jnp.maximum(peak_a, peak_b)
    factor_a = jnp.exp(peak_a - highest)
    factor_b = jnp.exp(peak_b - highest)
    return (
        highest,
        mass_a * factor_a + mass_b * factor_b,
        accum_a * factor_a[..., None] + accum_b * factor_b[..., None],
    )


def per_device(
    token_ids,
    request_order,
    cache_lengths,
    embed_table,
    attn_gain,
    proj_query,
    proj_kv,
    kv_cache,
    proj_out,
    mlp_gain,
    proj_gate,
    proj_up,
    proj_down,
):
    n_req, n_steps = token_ids.shape
    width = proj_query.shape[0]
    head_dim = kv_cache.shape[-1] // 2
    group_heads = proj_query.shape[1] // head_dim
    ctx_dev = kv_cache.shape[1]
    columns = embed_table.shape[1]
    vocab_rows = embed_table.shape[0]
    scale = head_dim ** (-0.5)
    owners = lax.axis_size("tok") * lax.axis_size("kv")
    owner_index = lax.axis_index("tok") * lax.axis_size("kv") + lax.axis_index("kv")
    seq_rank = lax.axis_index("seq")
    offset = token_ids.reshape(-1) - owner_index * vocab_rows
    inside = (offset >= 0) & (offset < vocab_rows)
    picked = jnp.take(embed_table, jnp.clip(offset, 0, vocab_rows - 1), axis=0)
    partial_x = jnp.where(inside[:, None], picked.astype(jnp.float32), 0.0)
    local_x = lax.psum(partial_x.astype(jnp.bfloat16), ("tok", "kv"))
    kv_flat = proj_kv.reshape(width, -1)
    full_x = lax.all_gather(local_x, "seq", axis=1, tiled=True)
    widened = full_x.astype(jnp.float32)
    square_mean = jnp.mean(widened * widened, axis=1)
    scaled = (widened * attn_gain.astype(jnp.float32)).astype(jnp.bfloat16)
    q_raw = jnp.dot(scaled, proj_query, preferred_element_type=jnp.float32)
    kv_raw = jnp.dot(scaled, kv_flat, preferred_element_type=jnp.float32)
    inv_norm = lax.rsqrt(square_mean + EPSILON)[:, None]
    q_scaled = (q_raw * inv_norm).reshape(n_req, n_steps, group_heads, head_dim)
    kv_scaled = (kv_raw * inv_norm).reshape(n_req, n_steps, 2 * head_dim)
    position = (cache_lengths[:, None] + jnp.arange(n_steps, dtype=jnp.int32)[None, :]).astype(
        jnp.float32
    )
    query = rotate(q_scaled, position[:, :, None]).astype(jnp.bfloat16)
    new_keys = rotate(kv_scaled[..., :head_dim], position).astype(jnp.bfloat16)
    new_values = kv_scaled[..., head_dim:].astype(jnp.bfloat16)
    cache_rows = kv_cache[:, :, 0, :]
    key_part = cache_rows[..., :head_dim]
    value_part = cache_rows[..., head_dim:]
    scores = (
        jnp.einsum("rjgd,rpd->rjgp", query, key_part, preferred_element_type=jnp.float32) * scale
    )
    places = seq_rank * ctx_dev + jnp.arange(ctx_dev, dtype=jnp.int32)
    is_live = (places[None, :] < cache_lengths[:, None])[:, None, None, :]
    masked = jnp.where(is_live, scores, FLOOR_SCORE)
    block_peak = jnp.max(masked, axis=-1)
    block_weight = jnp.where(is_live, jnp.exp(masked - block_peak[..., None]), 0.0).astype(
        jnp.bfloat16
    )
    block_mass = jnp.sum(block_weight.astype(jnp.float32), axis=-1)
    block_accum = jnp.einsum(
        "rjgp,rpd->rjgd", block_weight, value_part, preferred_element_type=jnp.float32
    )
    peak_all, mass_all, accum_all = combined_all(
        (block_peak, block_mass, block_accum), "seq", combine
    )
    fresh_scores = (
        jnp.einsum("rjgd,rkd->rjgk", query, new_keys, preferred_element_type=jnp.float32) * scale
    )
    causal = (jnp.arange(n_steps)[:, None] >= jnp.arange(n_steps)[None, :])[None, :, None, :]
    fresh_masked = jnp.where(causal, fresh_scores, FLOOR_SCORE)
    fresh_peak = jnp.max(fresh_masked, axis=-1)
    fresh_weight = jnp.where(causal, jnp.exp(fresh_masked - fresh_peak[..., None]), 0.0).astype(
        jnp.bfloat16
    )
    fresh_mass = jnp.sum(fresh_weight.astype(jnp.float32), axis=-1)
    fresh_accum = jnp.einsum(
        "rjgk,rkd->rjgd", fresh_weight, new_values, preferred_element_type=jnp.float32
    )
    highest = jnp.maximum(peak_all, fresh_peak)
    cache_factor = jnp.exp(peak_all - highest)
    fresh_factor = jnp.exp(fresh_peak - highest)
    numer = accum_all * cache_factor[..., None] + fresh_accum * fresh_factor[..., None]
    denom = mass_all * cache_factor + fresh_mass * fresh_factor
    attended = (
        (numer / denom[..., None])
        .astype(jnp.bfloat16)
        .reshape(n_req, n_steps, group_heads * head_dim)
    )
    slot_rows = attended[request_order].reshape(n_req * n_steps, group_heads * head_dim)
    per_owner = n_req // owners
    attn_part = lax.psum_scatter(
        jnp.dot(slot_rows, proj_out, preferred_element_type=jnp.float32),
        ("tok", "kv"),
        scatter_dimension=0,
        tiled=True,
    )
    my_requests = lax.dynamic_slice_in_dim(request_order, owner_index * per_owner, per_owner)
    own_x = local_x.reshape(n_req, n_steps, columns)[my_requests].reshape(
        per_owner * n_steps, columns
    )
    mid = (own_x.astype(jnp.float32) + attn_part).astype(jnp.bfloat16)
    piece_wide = lax.all_gather(mid, "seq", axis=1, tiled=True).astype(jnp.float32)
    gain_part = mlp_gain.astype(jnp.float32)
    piece_scaled = (piece_wide * gain_part).astype(jnp.bfloat16)
    gate_acc = jnp.dot(piece_scaled, proj_gate, preferred_element_type=jnp.float32)
    up_acc = jnp.dot(piece_scaled, proj_up, preferred_element_type=jnp.float32)
    square_total = jnp.sum(piece_wide * piece_wide, axis=1)
    inv_mlp = lax.rsqrt(square_total / width + EPSILON)[:, None]
    hidden = (jax.nn.silu(gate_acc * inv_mlp) * (up_acc * inv_mlp)).astype(jnp.bfloat16)
    down_terms = jnp.dot(hidden, proj_down, preferred_element_type=jnp.float32)
    mlp_part = lax.psum_scatter(down_terms, "seq", scatter_dimension=1, tiled=True)
    result = (mid.astype(jnp.float32) + mlp_part).astype(jnp.bfloat16)
    return result.reshape(per_owner, n_steps, columns)


def solution(mesh):
    placed = (
        P(),
        P(),
        P(),
        P(("tok", "kv"), "seq"),
        P(),
        P(None, ("tok", "kv")),
        P(None, ("tok", "kv"), None),
        P(None, "seq", ("tok", "kv"), None),
        P(("tok", "kv"), "seq"),
        P(),
        P(None, "seq"),
        P(None, "seq"),
        P("seq", None),
    )
    return jax.shard_map(
        per_device,
        mesh=mesh,
        in_specs=placed,
        out_specs=P(("tok", "kv"), None, "seq"),
        check_vma=False,
    )
```

profile of v0, /device:TPU:0, one launch (start us, length us, event | category | flops | bytes accessed | tf_op | source)
XLA Modules:
  0.0 429.5 jit_solution(7146980658867892863)
XLA Ops:
  11.6 61.3 %all-reduce.2.cloned.1.call-done = bf16[256,128]{1,0:T(8,128)(2,1)} async-done(((bf16[256,128]{1,0:T(8,128)(2,1)}), bf16[256,128]{1,0:T(8,128)(2,1)}) %all-reduce.2.cloned.1.call-update) | async-done | bytes 65552 | tf_op jit(solution)/shard_map/psum | solution.py:76
  73.6 22.1 %copy.87 = bf16[64,1024,1,128]{1,3,0,2:T(8,128)(2,1)} copy(bf16[64,1024,1,128]{3,1,2,0:T(8,128)(2,1)} %param.22) | data formatting | bytes 33554432 | tf_op args[7]
  96.5 21.2 %all-gather.6.cloned.1.call-done = bf16[256,2048]{1,0:T(8,128)(2,1)} async-done(((bf16[256,128]{1,0:T(8,128)(2,1)}), bf16[256,2048]{1,0:T(8,128)(2,1)}) %all-gather.6.cloned.1.call-update) | async-done | bytes 1048592 | tf_op jit(solution)/shard_map/all_gather | solution.py:78
  125.2 6.2 %fusion.5 = (f32[64,4,4]{2,1,0:T(4,128)S(1)}, f32[64,4,4,1024]{3,2,1,0:T(4,128)S(1)}) fusion(pred[64,1024]{1,0:T(8,128)(4,1)} %broadcast_compare_fusion, bf16[64,1024,128]{1,2,0:T(8,128)(2,1)} %bitcast.67, bf16[64,4,4,32]{3,2,1,0:T(4,128)(2,1)S(1)} %get-tuple-element.101, bf16[64,4,4,32]{3,2,1,0:T(4,128)(2,1)S(1)} %get-tuple-element.100), kind=kOutput, calls=%fused_computation.18 | convolution fusion | flops 137624576 | bytes 12783616 | tf_op jit(solution)/shard_map/rjgd,rpd->rjgp/dot_general | solution.py:97
  131.4 3.7 convert_reduce_fusion
  135.1 6.8 %fusion.3 = f32[64,4,4,64]{3,2,1,0:T(4,128)} fusion(bf16[64,4,4,1024]{3,2,1,0:T(4,128)(2,1)S(1)} %get-tuple-element.99, bf16[64,1024,128]{1,2,0:T(8,128)(2,1)} %bitcast.68), kind=kOutput, calls=%fused_computation.12 | convolution fusion | flops 134217728 | bytes 10747904 | tf_op jit(solution)/shard_map/rjgp,rpd->rjgd/dot_general | solution.py:107
  142.7 30.8 %all-gather.1 = f32[1024,4,4]{2,1,0:T(4,128)S(1)} all-gather(f32[64,4,4]{2,1,0:T(4,128)S(1)} %get-tuple-element.98), channel_id=3, replica_groups=mesh['tok'=4,'seq'=16,'kv'=2] {'seq'}, dimensions={0}, use_global_device_ids=true | all-gather | bytes 69632 | tf_op jit(solution)/shard_map/all_gather | solution.py:12
  174.9 32.0 %all-gather = f32[1024,4,4]{2,1,0:T(4,128)S(1)} all-gather(f32[64,4,4]{2,1,0:T(4,128)S(1)} %get-tuple-element.110), channel_id=2, replica_groups=mesh['tok'=4,'seq'=16,'kv'=2] {'seq'}, dimensions={0}, use_global_device_ids=true | all-gather | bytes 69632 | tf_op jit(solution)/shard_map/all_gather | solution.py:12
  209.1 3.3 fusion.36
  214.6 2.7 copy.93
  219.6 5.8 %all-gather.8.cloned.1.call-done = f32[1024,4,4,64]{3,2,1,0:T(4,128)} async-done(((f32[64,4,4,64]{3,2,1,0:T(4,128)}), f32[1024,4,4,64]{3,2,1,0:T(4,128)}) %all-gather.8.cloned.1.call-update) | async-done | bytes 4194320 | tf_op jit(solution)/shard_map/all_gather | solution.py:12
  225.3 7.7 %slice.77 = f32[960,4,4,64]{3,2,1,0:T(4,128)} slice(f32[1024,4,4,64]{3,2,1,0:T(4,128)} %all-gather.8.cloned.1.call-done), slice={[64:1024], [0:4], [0:4], [0:64]} | slice | bytes 7864320 | tf_op jit(solution)/shard_map/slice | solution.py:14
  233.1 53.9 %while.14 = (s32[]{:T(128)}, f32[64,4,4]{0,2,1:T(4,128)S(1)}, f32[64,4,4]{0,2,1:T(4,128)S(1)}, f32[64,4,4,64]{3,2,1,0:T(4,128)S(1)}, f32[15,64,4,4]{1,3,2,0:T(4,...) while((s32[]{:T(128)}, f32[64,4,4]{0,2,1:T(4,128)S(1)}, ...), condition=%wide.region_5.6_spmd, body=%wide.region_4.5_spmd.sunk | while | flops 202754 | bytes 843877 | solution.py:15
  234.1 2.6 fusion.54
  237.7 2.6 fusion.54
  241.3 2.6 fusion.54
  244.9 2.6 fusion.54
  248.5 2.6 fusion.54
  252.1 2.6 fusion.54
  255.7 2.6 fusion.54
  259.2 2.6 fusion.54
  262.8 2.6 fusion.54
  266.4 2.6 fusion.54
  270.0 2.6 fusion.54
  273.6 2.6 fusion.54
  277.2 2.6 fusion.54
  280.8 2.6 fusion.54
  284.4 2.6 fusion.54
  294.2 28.4 %reduce-scatter.3.cloned.1.call-done = f32[32,128]{1,0:T(8,128)} async-done(((f32[256,128]{1,0:T(8,128)}), f32[32,128]{1,0:T(8,128)}) %reduce-scatter.3.cloned.1.call-update) | async-done | bytes 16400 | tf_op jit(solution)/shard_map/reduce_scatter | solution.py:138
  323.3 23.8 %all_gather.31 = bf16[32,2048]{1,0:T(8,128)(2,1)S(1)} all-gather(bf16[32,128]{1,0:T(8,128)(2,1)S(1)} %fusion.32), channel_id=1, replica_groups=mesh['tok'=4,'seq'=16,'kv'=2] {'seq'}, dimensions={1}, use_global_device_ids=true | all-gather | bytes 139264 | tf_op jit(solution)/shard_map/all_gather | solution.py:149
  349.3 3.2 fusion.13
  352.6 69.1 %reduce-scatter.5.cloned.1.call-done = f32[32,128]{1,0:T(8,128)} async-done(((f32[32,2048]{1,0:T(8,128)}), f32[32,128]{1,0:T(8,128)}) %reduce-scatter.5.cloned.1.call-update) | async-done | bytes 16400 | tf_op jit(solution)/shard_map/reduce_scatter | solution.py:158
  (142 shorter events, 49.0 us)
Async XLA Ops:
  6.5 342.8 %copy-start = (bf16[512,2048]{1,0:T(8,128)(2,1)S(1)}, bf16[512,2048]{1,0:T(8,128)(2,1)}, u32[]{:S(2)}) copy-start(bf16[512,2048]{1,0:T(8,128)(2,1)} %param.27) | copy-start | bytes 6291460
  6.5 66.3 %all-reduce.2.cloned.1.call-start = ((), (), s32[]{:S(2)}) async-start(), calls=%async_computation.2 | async-start | bytes 131072 | tf_op jit(solution)/shard_map/psum | solution.py:76
  11.5 106.1 %all-gather.6.cloned.1.call-start = ((), (), s32[]{:S(2)}) async-start(), calls=%async_computation.3 | async-start | bytes 1114112 | tf_op jit(solution)/shard_map/all_gather | solution.py:78
  72.9 152.4 %all-gather.8.cloned.1.call-start = ((), (), s32[]{:S(2)}) async-start(), calls=%async_computation.6 | async-start | bytes 8912896 | tf_op jit(solution)/shard_map/all_gather | solution.py:12
  73.6 22.1 %copy-start.7 = (s32[64]{0:T(128)S(1)}, s32[64]{0:T(128)}, u32[]{:S(2)}) copy-start(s32[64]{0:T(128)} %param.17) | copy-start | bytes 772
  125.2 6.2 %copy-start.1 = (pred[64,1024]{1,0:T(8,128)(4,1)S(1)}, pred[64,1024]{1,0:T(8,128)(4,1)}, u32[]{:S(2)}) copy-start(pred[64,1024]{1,0:T(8,128)(4,1)} %broadcast_compare_fusion) | copy-start | bytes 196612
  135.1 6.9 %copy-start.9 = (s32[64]{0:T(128)S(1)}, s32[64]{0:T(128)}, u32[]{:S(2)}) copy-start(s32[64]{0:T(128)} %param.16) | copy-start | bytes 772
  142.0 180.6 %reduce-scatter.3.cloned.1.call-start = ((), (), s32[]{:S(2)}) async-start(), calls=%async_computation.4 | async-start | bytes 147456 | tf_op jit(solution)/shard_map/reduce_scatter | solution.py:138
  142.1 70.6 %copy-start.8 = (pred[4,4]{1,0:T(4,128)(4,1)}, pred[4,4]{1,0:T(4,128)(4,1)S(1)}, u32[]{:S(2)}) copy-start(pred[4,4]{1,0:T(4,128)(4,1)S(1)} %iota_compare_fusion) | copy-start | bytes 52
  174.9 33.4 %copy-start.3 = (bf16[64,4,32]{0,2,1:T(8,128)(2,1)S(1)}, bf16[64,4,32]{0,2,1:T(8,128)(2,1)}, u32[]{:S(2)}) copy-start(bf16[64,4,32]{0,2,1:T(8,128)(2,1)} %get-tuple-element.108) | copy-start | bytes 49156
  174.9 33.4 %copy-start.4 = (bf16[64,4,32]{0,2,1:T(8,128)(2,1)S(1)}, bf16[64,4,32]{0,2,1:T(8,128)(2,1)}, u32[]{:S(2)}) copy-start(bf16[64,4,32]{0,2,1:T(8,128)(2,1)} %get-tuple-element.109) | copy-start | bytes 49156
  225.3 7.7 %slice-start = ((f32[1024,4,4,64]{3,2,1,0:T(4,128)}), f32[64,4,4,64]{3,2,1,0:T(4,128)S(1)}, s32[]{:S(2)}) async-start(f32[1024,4,4,64]{3,2,1,0:T(4,128)} %all-gather.8.cloned.1.call-done), calls=%async_computation.7 | async-start | bytes 1048576 | tf_op jit(solution)/shard_map/slice | solution.py:13
  233.1 55.7 %copy-start.2 = (bf16[64,4,4,4]{3,2,1,0:T(4,128)(2,1)S(1)}, bf16[64,4,4,4]{3,2,1,0:T(4,128)(2,1)}, u32[]{:S(2)}) copy-start(bf16[64,4,4,4]{3,2,1,0:T(4,128)(2,1)} %copy.102) | copy-start | bytes 24580
  288.7 3.1 copy-start.5
  288.7 4.0 copy-start.6
  288.7 4.0 copy-start.10
  292.6 129.0 %reduce-scatter.5.cloned.1.call-start = ((), (), s32[]{:S(2)}) async-start(), calls=%async_computation.5 | async-start | bytes 278528 | tf_op jit(solution)/shard_map/reduce_scatter | solution.py:158
Sparse Core Ops, SparseCore 0:
  11.7 61.1 all-reduce.1
  75.2 42.4 all-gather.5
  142.1 83.1 all-gather.7
  292.8 29.7 reduce-scatter.2
  352.7 68.9 reduce-scatter.4
where the time goes:
time: 432 us; the launch traced here: 430 us
  waiting for transfers between devices  186 us (43%)
  blocking collectives  86.6 us (20%)
  other arithmetic  63.8 us (15%)
  local copies, waits for them, and re-layouts  51.2 us (12%)
  matrix products  28.1 us (7%)
  between operations  13.4 us (3%)
    reduce_scatter x1, waiting for transfers between devices, per_device(): lax.psum_scatter(down_terms, 'seq', scatter_dimension=1, tiled=True)  69.1 us
    all_gather x2, blocking collectives, combined_all(): pieces = jax.tree.map(lambda part: lax.all_gather(part, axis), value)  62.8 us
    psum x1, waiting for transfers between devices, per_device(): local_x = lax.psum(partial_x.astype(jnp.bfloat16), ('tok', 'kv'))  61.3 us
    add x15, other arithmetic, combine(): accum_a * factor_a[..., None] + accum_b * factor_b[..., None]  38.7 us
    reduce_scatter x1, waiting for transfers between devices, per_device(): lax.psum_scatter(jnp.dot(slot_rows, proj_out, preferred_element_type=jnp....  28.4 us
    all_gather x1, blocking collectives, per_device(): lax.all_gather(mid, 'seq', axis=1, tiled=True).astype(jnp.float32)  23.8 us
    unnamed x25, local copies, waits for them, and re-layouts  22.3 us
    all_gather x1, waiting for transfers between devices, per_device(): full_x = lax.all_gather(local_x, 'seq', axis=1, tiled=True)  21.2 us
  transfers between devices with their start and end apart: 5, of which 5 were waited for; matrix products, arithmetic and copies ran while one was open for 9% of the time, Pallas kernels for 0%

commit v1 on v0

v1 whole, which is shorter than its diff:
```python
import functools

import jax
import jax.numpy as jnp
import numpy as np
from jax import lax
from jax.experimental import pallas as pl
from jax.experimental.pallas import tpu as pltpu
from jax.sharding import PartitionSpec as P

EPSILON = 1e-05
ROPE_BASE = 1000000.0
FLOOR_SCORE = -1e30
MESH = pl.DeviceIdType.MESH
F32 = jnp.float32
BF16 = jnp.bfloat16


def iota(shape, dim):
    return lax.broadcasted_iota(jnp.int32, shape, dim)


def dot_nt(a, b):
    return lax.dot_general(a, b, (((1,), (1,)), ((), ())), preferred_element_type=F32)


def dot(a, b):
    return jnp.dot(a, b, preferred_element_type=F32)


def layer_kernel(
    n_tok,
    n_seq,
    n_kv,
    ids_ref,
    order_ref,
    len_ref,
    gain_ref,
    freq_ref,
    table_hbm,
    wq_hbm,
    wkv_hbm,
    cache_hbm,
    wo_hbm,
    wg_hbm,
    wu_hbm,
    wd_hbm,
    out_ref,
    table,
    wq,
    wkv,
    cache,
    wo,
    wg,
    wu,
    wd,
    ids_v,
    x_send,
    x_recv,
    x_all,
    x_rows,
    q_all,
    q_rows,
    s_scr,
    p_scr,
    acc_send,
    acc_recv,
    st_send,
    st_recv,
    st_t,
    at_all,
    o_send,
    o_recv,
    mid_all,
    d_send,
    d_recv,
    load_sem,
    send_sem,
    yc_sem,
    seq_sem,
):
    n_own = n_tok * n_kv
    tok = lax.axis_index("tok")
    seq = lax.axis_index("seq")
    kv = lax.axis_index("kv")
    own = tok * n_kv + kv
    vocab = table.shape[0]
    ctx = cache.shape[1]
    n_req = cache.shape[0]
    steps = 4
    rows_own = x_all.shape[1]
    rows_seq = x_rows.shape[1]
    slots_seq = rows_seq // steps

    def seq_peer(s):
        return (tok, s, kv)

    def own_peer(g):
        return (g // n_kv, seq, lax.rem(g, n_kv))

    barrier = pltpu.get_barrier_semaphore()
    for d in range(1, n_own):
        pl.semaphore_signal(
            barrier, inc=1, device_id=own_peer(lax.rem(own + d, n_own)), device_id_type=MESH
        )
    for d in range(1, n_seq):
        pl.semaphore_signal(
            barrier, inc=1, device_id=seq_peer(lax.rem(seq + d, n_seq)), device_id_type=MESH
        )

    loads = []

    def load(src, dst):
        copy = pltpu.make_async_copy(src, dst, load_sem.at[len(loads)])
        copy.start()
        loads.append(copy)
        return copy

    table_load = load(table_hbm, table)
    wq_load = load(wq_hbm, wq)
    wkv_load = load(wkv_hbm, wkv)
    chunk = 8
    cache_loads = [
        load(cache_hbm.at[pl.ds(c, chunk)], cache.at[pl.ds(c, chunk)])
        for c in range(0, n_req, chunk)
    ]
    wo_load = load(wo_hbm, wo)
    wg_load = load(wg_hbm, wg)
    wu_load = load(wu_hbm, wu)
    wd_load = load(wd_hbm, wd)

    def own_copy(phase, src, dst, g):
        return pltpu.make_async_remote_copy(
            src_ref=src,
            dst_ref=dst,
            send_sem=send_sem.at[phase],
            recv_sem=yc_sem.at[phase, own],
            device_id=own_peer(g),
            device_id_type=MESH,
        )

    def seq_copy(phase, src, dst, s):
        return pltpu.make_async_remote_copy(
            src_ref=src,
            dst_ref=dst,
            send_sem=send_sem.at[phase + 3],
            recv_sem=seq_sem.at[phase, seq],
            device_id=seq_peer(s),
            device_id_type=MESH,
        )

    def own_wait(phase, dst):
        for d in range(1, n_own):
            g = lax.rem(own + d, n_own)
            pltpu.make_async_copy(dst.at[g], dst.at[g], yc_sem.at[phase, g]).wait()

    def seq_wait(phase, dst, s):
        pltpu.make_async_copy(dst.at[s], dst.at[s], seq_sem.at[phase, s]).wait()

    def seq_wait_all(phase, dst):
        for d in range(1, n_seq):
            seq_wait(phase, dst, lax.rem(seq + d, n_seq))

    def sent(index, buffer, count):
        part = buffer.at[pl.ds(0, count)]
        pltpu.make_async_copy(part, part, send_sem.at[index]).wait()

    sub8 = iota((8, 128), 0)

    def ids_block(b, carry):
        value = jnp.zeros((8, 128), jnp.int32)
        for i in range(8):
            request = order_ref[b * 2 + i // steps]
            value = jnp.where(sub8 == i, ids_ref[i % steps, request], value)
        ids_v[pl.ds(pl.multiple_of(b * 8, 8), 8), :] = value
        return carry

    lax.fori_loop(0, n_req * steps // 8, ids_block, 0)

    table_load.wait()
    kt = 512
    n_rows = n_req * steps
    wide_ids = jnp.concatenate([ids_v[...]] * (kt // 128), axis=1) - own * vocab
    lane_k = iota((n_rows, kt), 1)

    def pick(c, acc):
        hot = jnp.where(wide_ids == lane_k + c * kt, 1.0, 0.0).astype(BF16)
        return acc + dot(hot, table[pl.ds(pl.multiple_of(c * kt, kt), kt), :])

    picked = lax.fori_loop(0, vocab // kt, pick, jnp.zeros((n_rows, 128), F32)).astype(BF16)
    x_send[...] = picked.reshape(n_own, rows_own, 128)

    pl.semaphore_wait(barrier, n_own - 1 + n_seq - 1)

    for d in range(1, n_own):
        g = lax.rem(own + d, n_own)
        own_copy(0, x_send.at[g], x_recv.at[own], g).start()
    x_recv[own] = x_send[own]
    own_wait(0, x_recv)
    x_own = x_recv[0].astype(F32)
    for g in range(1, n_own):
        x_own = x_own + x_recv[g].astype(F32)

    x_all[own] = x_own.astype(BF16)
    for d in range(1, n_own):
        g = lax.rem(own + d, n_own)
        own_copy(1, x_all.at[own], x_all.at[own], g).start()
    own_wait(1, x_all)

    per = rows_own // rows_seq

    def seq_rows(s):
        return x_all.at[s // per, pl.ds(pl.multiple_of(lax.rem(s, per) * rows_seq, rows_seq), rows_seq)]

    for d in range(1, n_seq):
        s = lax.rem(seq + d, n_seq)
        seq_copy(0, seq_rows(s), x_rows.at[seq], s).start()
    x_rows[seq] = seq_rows(seq)[...]

    row16 = iota((rows_seq, 128), 0)
    lane16 = iota((rows_seq, 128), 1)
    base_pos = jnp.zeros((rows_seq, 128), jnp.int32)
    for i in range(slots_seq):
        length = len_ref[order_ref[seq * slots_seq + i]]
        base_pos = jnp.where(row16 // steps == i, length, base_pos)
    position = (base_pos + lax.rem(row16, steps)).astype(F32)
    angle = position * freq_ref[...]
    turns = jnp.round(angle * (1.0 / (2.0 * np.pi)))
    angle = angle - turns * 6.28125
    angle = angle - turns * 0.0019350051879882812
    angle = angle - turns * 3.0199159819e-07
    cosine = jnp.cos(angle)
    sine = jnp.sin(angle)
    front = lax.rem(lane16, 64) < 32

    def rotate(v):
        swapped = jnp.where(front, -pltpu.roll(v, 96, 1), pltpu.roll(v, 32, 1))
        return v * cosine + swapped * sine

    seq_wait_all(0, x_rows)
    width = n_seq * 128
    x16 = jnp.concatenate([x_rows[s] for s in range(n_seq)], axis=1).astype(F32)
    inv_attn = lax.rsqrt(jnp.sum(x16 * x16, axis=1, keepdims=True) / width + EPSILON)
    scaled = (x16 * gain_ref[0:1, :]).astype(BF16)
    wq_load.wait()
    wkv_load.wait()
    q_raw = dot(scaled, wq[...]) * inv_attn
    kv_raw = dot(scaled, wkv[...]) * inv_attn
    q_tiles = [rotate(q_raw[:, t * 128 : (t + 1) * 128]).astype(BF16) for t in range(2)]
    low = lane16 < 64
    fresh = jnp.where(low, rotate(kv_raw), kv_raw).astype(BF16).astype(F32)
    q_all[seq] = jnp.concatenate(q_tiles, axis=1)
    for d in range(1, n_seq):
        s = lax.rem(seq + d, n_seq)
        seq_copy(1, q_all.at[seq], q_all.at[seq], s).start()

    key_lo = jnp.where(low, fresh, 0.0)
    val_hi = jnp.where(low, 0.0, fresh)
    keys = [key_lo.astype(BF16), pltpu.roll(key_lo, 64, 1).astype(BF16)]
    values = [pltpu.roll(val_hi, 64, 1).astype(BF16), val_hi.astype(BF16)]
    r_i = iota((rows_seq, rows_seq), 0)
    c_i = iota((rows_seq, rows_seq), 1)
    causal = (r_i // steps == c_i // steps) & (c_i <= r_i)
    f_peak, f_mass, f_acc = [], [], []
    for h in range(4):
        t = jnp.where(causal, dot_nt(q_tiles[h // 2], keys[h % 2]) * 0.125, FLOOR_SCORE)
        peak = jnp.max(t, axis=1, keepdims=True)
        w = jnp.where(causal, jnp.exp(t - peak), 0.0).astype(BF16)
        f_peak.append(peak)
        f_mass.append(jnp.sum(w.astype(F32), axis=1, keepdims=True))
        f_acc.append(dot(w, values[h % 2]))

    for c in cache_loads:
        c.wait()
    seq_wait_all(1, q_all)

    group = 8
    n_group = n_req // group
    pt = 256
    lane_slot = lax.rem(iota((1, 128), 1), group * steps) // steps
    row_slot = lax.rem(iota((128, 128), 0), group * steps) // steps
    lane32 = iota((group * steps, 128), 1)
    value_slot = lax.rem(iota((128, 256), 0), group * steps) // steps

    def attend(k, carry):
        grp = lax.rem(seq // 2 + 1 + k, n_group)
        q32 = q_all[pl.ds(grp * 2, 2)].reshape(group * steps, 256).astype(F32)
        pieces = []
        for h in range(4):
            tile = q32[:, (h // 2) * 128 : (h // 2 + 1) * 128]
            if h % 2:
                tile = pltpu.roll(tile, 64, 1)
            pieces.append(jnp.where(lane32 < 64, tile, 0.0))
        q128 = jnp.concatenate(pieces, axis=0) * 0.125
        requests = [order_ref[grp * group + r] for r in range(group)]
        lengths = jnp.zeros((1, 128), jnp.int32)
        for r in range(group):
            lengths = jnp.where(lane_slot == r, len_ref[requests[r]], lengths)
        lengths = lengths - seq * ctx
        rhs = jnp.concatenate(
            [jnp.where(row_slot == r, q128, 0.0).astype(BF16) for r in range(group)], axis=1
        )
        q_rows[...] = rhs
        peak = jnp.full((1, 128), FLOOR_SCORE, F32)
        for t in range(ctx // pt):
            lhs = jnp.concatenate(
                [cache[requests[r], t * pt : (t + 1) * pt, :] for r in range(group)], axis=1
            )
            scores = dot_nt(lhs, q_rows[...])
            live = iota((pt, 128), 0) + t * pt < lengths
            scores = jnp.where(live, scores, FLOOR_SCORE)
            s_scr[t * pt : (t + 1) * pt, :] = scores
            peak = jnp.maximum(peak, jnp.max(scores, axis=0, keepdims=True))
        mass = jnp.zeros((1, 128), F32)
        for t in range(ctx // pt):
            live = iota((pt, 128), 0) + t * pt < lengths
            w = jnp.exp(s_scr[t * pt : (t + 1) * pt, :] - peak)
            w = jnp.where(live, w, 0.0).astype(BF16)
            mass = mass + jnp.sum(w.astype(F32), axis=0, keepdims=True)
            p_scr[:, t * pt : (t + 1) * pt] = w.T
        total = jnp.zeros((128, 128), F32)
        for r in range(0, group, 2):
            both = jnp.concatenate([cache[requests[r]], cache[requests[r + 1]]], axis=1)
            both = dot(p_scr[...], both)
            total = jnp.where(row_slot == r, both[:, :128], total)
            total = jnp.where(row_slot == r + 1, both[:, 128:], total)
        st_send[grp] = jnp.concatenate([peak, mass], axis=0)
        for pair in range(2):
            even = pltpu.roll(total[pair * 64 : pair * 64 + 32], 64, 1)
            tile = jnp.where(lane32 < 64, even, total[pair * 64 + 32 : pair * 64 + 64])
            for a in range(2):
                acc_send[grp * 2 + a, pair * rows_seq : (pair + 1) * rows_seq] = tile[
                    a * rows_seq : (a + 1) * rows_seq
                ].astype(BF16)
        for a in range(2):
            s = grp * 2 + a

            @pl.when(s != seq)
            def _():
                seq_copy(2, acc_send.at[s], acc_recv.at[seq], s).start()
                seq_copy(3, st_send.at[grp], st_recv.at[seq], s).start()

        return carry

    lax.fori_loop(0, n_group, attend, 0)

    acc_recv[seq] = acc_send[seq]
    st_recv[seq] = st_send[seq // 2]
    seq_wait_all(3, st_recv)
    stats = jnp.concatenate([st_recv[:, 0, :], st_recv[:, 1, :]], axis=0)
    st_t[...] = jnp.concatenate([stats, jnp.zeros((128 - 2 * n_seq, 128), F32)], axis=0).T
    shares, f_share = [], []
    for h in range(4):
        offset = pl.multiple_of(h * 32 + lax.rem(seq, 2) * rows_seq, rows_seq)
        block = st_t[pl.ds(offset, rows_seq), :]
        peaks, masses = block[:, :n_seq], block[:, n_seq : 2 * n_seq]
        top = jnp.maximum(jnp.max(peaks, axis=1, keepdims=True), f_peak[h])
        factor = jnp.exp(peaks - top)
        f_factor = jnp.exp(f_peak[h] - top)
        denom = jnp.sum(factor * masses, axis=1, keepdims=True) + f_factor * f_mass[h]
        shares.append(factor / denom)
        f_share.append(f_factor / denom)
    tiles = []
    for pair in range(2):
        tiles.append(f_acc[2 * pair] * f_share[2 * pair] + f_acc[2 * pair + 1] * f_share[2 * pair + 1])
    seq_wait_all(2, acc_recv)
    for s in range(n_seq):
        part = acc_recv[s].astype(F32)
        for pair in range(2):
            weight = jnp.where(low, shares[2 * pair][:, s : s + 1], shares[2 * pair + 1][:, s : s + 1])
            tiles[pair] = tiles[pair] + weight * part[pair * rows_seq : (pair + 1) * rows_seq]

    at_all[seq] = jnp.concatenate([t.astype(BF16) for t in tiles], axis=1)
    for d in range(1, n_seq):
        s = lax.rem(seq + d, n_seq)
        seq_copy(4, at_all.at[seq], at_all.at[seq], s).start()
    wo_load.wait()
    seq_wait_all(4, at_all)
    partial = dot(at_all[...].reshape(n_rows, 256), wo[...]).astype(BF16)
    o_send[...] = partial.reshape(n_own, rows_own, 128)
    for d in range(1, n_own):
        g = lax.rem(own + d, n_own)
        own_copy(2, o_send.at[g], o_recv.at[own], g).start()
    o_recv[own] = o_send[own]
    own_wait(2, o_recv)
    attn = o_recv[0].astype(F32)
    for g in range(1, n_own):
        attn = attn + o_recv[g].astype(F32)
    mid = (x_own + attn).astype(BF16)
    mid_all[seq] = mid
    for d in range(1, n_seq):
        s = lax.rem(seq + d, n_seq)
        seq_copy(5, mid_all.at[seq], mid_all.at[seq], s).start()

    wg_load.wait()
    wu_load.wait()
    seq_wait_all(5, mid_all)
    m = jnp.concatenate([mid_all[s] for s in range(n_seq)], axis=1).astype(F32)
    inv_mlp = lax.rsqrt(jnp.sum(m * m, axis=1, keepdims=True) / width + EPSILON)
    scaled_mid = (m * gain_ref[1:2, :]).astype(BF16)
    gate = dot(scaled_mid, wg[...]) * inv_mlp
    up = dot(scaled_mid, wu[...]) * inv_mlp
    hidden = (gate / (1.0 + jnp.exp(-gate)) * up).astype(BF16)
    wd_load.wait()
    down = dot(hidden, wd[...]).astype(BF16)
    for s in range(n_seq):
        d_send[s] = down[:, s * 128 : (s + 1) * 128]
    for d in range(1, n_seq):
        s = lax.rem(seq + d, n_seq)
        seq_copy(6, d_send.at[s], d_recv.at[seq], s).start()
    d_recv[seq] = d_send[seq]
    seq_wait_all(6, d_recv)
    result = mid.astype(F32)
    for s in range(n_seq):
        result = result + d_recv[s].astype(F32)
    out_ref[...] = result.astype(BF16).reshape(out_ref.shape)

    sent(0, x_recv, n_own - 1)
    sent(1, x_all, n_own - 1)
    sent(2, o_recv, n_own - 1)
    sent(3, x_rows, n_seq - 1)
    sent(4, q_all, n_seq - 1)
    sent(5, acc_recv, n_seq - 1)
    sent(6, st_recv, n_seq - 1)
    sent(7, at_all, n_seq - 1)
    sent(8, mid_all, n_seq - 1)
    sent(9, d_recv, n_seq - 1)


def solution(mesh):
    n_tok, n_seq, n_kv = mesh.shape["tok"], mesh.shape["seq"], mesh.shape["kv"]
    n_own = n_tok * n_kv
    lanes = np.arange(128) % 32
    freq = (ROPE_BASE ** (-(lanes * 2.0 / 64))).astype(np.float32).reshape(1, 128)

    def per_device(
        token_ids,
        request_order,
        cache_lengths,
        embed_table,
        attn_gain,
        proj_query,
        proj_kv,
        kv_cache,
        proj_out,
        mlp_gain,
        proj_gate,
        proj_up,
        proj_down,
    ):
        n_req, steps = token_ids.shape
        ctx = kv_cache.shape[1]
        rows = n_req * steps
        r_own, r_seq = rows // n_own, rows // n_seq
        width = proj_query.shape[0]
        gains = jnp.stack([attn_gain, mlp_gain]).astype(F32)
        smem = pl.BlockSpec(memory_space=pltpu.SMEM)
        vmem = pl.BlockSpec(memory_space=pltpu.VMEM)
        hbm = pl.BlockSpec(memory_space=pl.ANY)
        weights = [
            embed_table,
            proj_query,
            proj_kv.reshape(width, 128),
            kv_cache.reshape(n_req, ctx, 128),
            proj_out,
            proj_gate,
            proj_up,
            proj_down,
        ]
        scratch = [pltpu.VMEM(w.shape, w.dtype) for w in weights]
        scratch += [
            pltpu.VMEM((rows, 128), jnp.int32),
            pltpu.VMEM((n_own, r_own, 128), BF16),
            pltpu.VMEM((n_own, r_own, 128), BF16),
            pltpu.VMEM((n_own, r_own, 128), BF16),
            pltpu.VMEM((n_seq, r_seq, 128), BF16),
            pltpu.VMEM((n_seq, r_seq, 256), BF16),
            pltpu.VMEM((128, 1024), BF16),
            pltpu.VMEM((ctx, 128), F32),
            pltpu.VMEM((128, ctx), BF16),
            pltpu.VMEM((n_seq, 2 * r_seq, 128), BF16),
            pltpu.VMEM((n_seq, 2 * r_seq, 128), BF16),
            pltpu.VMEM((n_req // 8, 2, 128), F32),
            pltpu.VMEM((n_seq, 2, 128), F32),
            pltpu.VMEM((128, 128), F32),
            pltpu.VMEM((n_seq, r_seq, 256), BF16),
            pltpu.VMEM((n_own, r_own, 128), BF16),
            pltpu.VMEM((n_own, r_own, 128), BF16),
            pltpu.VMEM((n_seq, r_own, 128), BF16),
            pltpu.VMEM((n_seq, r_own, 128), BF16),
            pltpu.VMEM((n_seq, r_own, 128), BF16),
            pltpu.SemaphoreType.DMA((16,)),
            pltpu.SemaphoreType.DMA((10,)),
            pltpu.SemaphoreType.DMA((3, n_own)),
            pltpu.SemaphoreType.DMA((7, n_seq)),
        ]
        return pl.pallas_call(
            functools.partial(layer_kernel, n_tok, n_seq, n_kv),
            out_shape=jax.ShapeDtypeStruct((n_req // n_own, steps, 128), BF16),
            in_specs=[smem, smem, smem, vmem, vmem] + [hbm] * len(weights),
            out_specs=vmem,
            scratch_shapes=scratch,
            compiler_params=pltpu.CompilerParams(
                collective_id=0, has_side_effects=True, vmem_limit_bytes=64 * 1000 * 1000
            ),
            name="layer",
        )(token_ids.T, request_order, cache_lengths, gains, jnp.asarray(freq), *weights)

    placed = (
        P(),
        P(),
        P(),
        P(("tok", "kv"), "seq"),
        P(),
        P(None, ("tok", "kv")),
        P(None, ("tok", "kv"), None),
        P(None, "seq", ("tok", "kv"), None),
        P(("tok", "kv"), "seq"),
        P(),
        P(None, "seq"),
        P(None, "seq"),
        P("seq", None),
    )
    return jax.shard_map(
        per_device,
        mesh=mesh,
        in_specs=placed,
        out_specs=P(("tok", "kv"), None, "seq"),
        check_vma=False,
    )
```

time: 432 us -> 67.4 us (0.16)
  waiting for transfers between devices: 186 us -> 0 us
  blocking collectives: 86.6 us -> 0 us
  Pallas kernels: 0 us -> 63.9 us
  other arithmetic: 63.8 us -> 0.62 us
  local copies, waits for them, and re-layouts: 51.2 us -> 2.69 us
  matrix products: 28.1 us -> 0 us
  between operations: 13.4 us -> 0.01 us
    reduce_scatter x2 -> x0, waiting for transfers between devices: 97.5 us -> none  [the longest x1 69.1 us: per_device(): lax.psum_scatter(down_terms, 'seq', scatter_dimension=1, tiled=True)]
    all_gather x3 -> x0, blocking collectives: 86.6 us -> none  [the longest x2 62.8 us: combined_all(): pieces = jax.tree.map(lambda part: lax.all_gather(part, axis), value)]
    pallas_call x0 -> x1, Pallas kernels: none -> 63.9 us  [per_device(): pl.pallas_call(functools.partial(layer_kernel, n_tok, n_seq, n_kv), out_s...]
    psum x1 -> x0, waiting for transfers between devices: 61.3 us -> none  [per_device(): local_x = lax.psum(partial_x.astype(jnp.bfloat16), ('tok', 'kv'))]
    add x32 -> x0, other arithmetic: 49.7 us -> none  [the longest x15 38.7 us: combine(): accum_a * factor_a[..., None] + accum_b * factor_b[..., None]]
    dot_general x9 -> x0, matrix products: 28.1 us -> none  [the longest x1 6.84 us: per_device(): jnp.einsum('rjgp,rpd->rjgd', block_weight, value_part, preferred_element_...]
    all_gather x2 -> x0, waiting for transfers between devices: 27 us -> none  [the longest x1 21.2 us: per_device(): full_x = lax.all_gather(local_x, 'seq', axis=1, tiled=True)]
    unnamed x25 -> x1, local copies, waits for them, and re-layouts: 22.3 us -> 1.3 us
  transfers between devices with their start and end apart: 5 -> 0, of which waited for: 5 -> 0; matrix products, arithmetic and copies ran while one was open for 9% -> 0% of each run, Pallas kernels for 0% -> 0%
where the time goes in v1:
time: 67.4 us; the launch traced here: 67.2 us
  Pallas kernels  63.9 us (95%)
  local copies, waits for them, and re-layouts  2.69 us (4%)
    pallas_call x1, Pallas kernels, per_device(): pl.pallas_call(functools.partial(layer_kernel, n_tok, n_seq, n_kv), out_s...  63.9 us
    another operation x2, local copies, waits for them, and re-layouts, per_device(): gains = jnp.stack([attn_gain, mlp_gain]).astype(F32)  1.39 us

profile of v1, /device:TPU:0, one launch (start us, length us, event | category | flops | bytes accessed | tf_op | source)
XLA Modules:
  0.0 67.2 jit_solution(2580561188746468442)
XLA Ops:
  0.0 0.7 %stack.9 = bf16[1,2048]{1,0:T(2,128)(2,1)S(1)} reshape(bf16[2048]{0:T(1024)(128)(2,1)} %param.18) | data formatting | bytes 8192 | tf_op jit(solution)/shard_map/stack | solution.py:456
  0.7 0.7 %stack.10 = bf16[1,2048]{1,0:T(2,128)(2,1)S(1)} reshape(bf16[2048]{0:T(1024)(128)(2,1)} %param.23) | data formatting | bytes 8192 | tf_op jit(solution)/shard_map/stack | solution.py:456
  1.4 0.6 maximum_convert_fusion.gain_ref
  2.0 63.9 %layer.1 = bf16[8,4,128]{2,1,0:T(4,128)(2,1)} custom-call(s32[4,64]{1,0:T(4,128)} %bitcast.5, s32[64]{0:T(128)} %order_ref.1, s32[64]{0:T(128)} %len_ref.1, f32[2,2048]{1,0:T(2,128)} %maximum_convert_fusion.gain_ref, f32[1,128]{1,0:T(1,128)} %constant.2.clone.freq_ref, bf16[4096,128]{1,0:T(8,128)(2,1)} %table_hbm.1, bf16[2048,256]{1,0:T(8,128)(2,1)} %wq_hbm.1, ...), custom_call_target="tpu_custom_call" | custom-call | tf_op jit(solution)/shard_map/layer/pallas_call | solution.py:497
  65.9 1.3 %copy.16 = bf16[8,4,128]{2,1,0:T(4,128)(2,1)} copy(bf16[8,4,128]{2,1,0:T(4,128)(2,1)} %layer.1) | data formatting | bytes 16384

commit v2 on v1

--- a/solution.py
+++ b/solution.py
@@ -26,6 +26,12 @@
 
 def dot(a, b):
     return jnp.dot(a, b, preferred_element_type=F32)
+
+
+def interleave(tiles, count, size):
+    return jnp.concatenate(
+        [t[i * size : (i + 1) * size] for i in range(count) for t in tiles], axis=0
+    )
 
 
 def layer_kernel(
@@ -36,6 +42,7 @@
     order_ref,
     len_ref,
     gain_ref,
+    gain2_ref,
     freq_ref,
     table_hbm,
     wq_hbm,
@@ -54,13 +61,15 @@
     wg,
     wu,
     wd,
+    keys,
+    vals,
+    gain2,
     ids_v,
     x_send,
     x_recv,
-    x_all,
+    x_own_v,
     x_rows,
     q_all,
-    q_rows,
     s_scr,
     p_scr,
     acc_send,
@@ -88,9 +97,12 @@
     ctx = cache.shape[1]
     n_req = cache.shape[0]
     steps = 4
-    rows_own = x_all.shape[1]
-    rows_seq = x_rows.shape[1]
+    n_rows = n_req * steps
+    rows_own = n_rows // n_own
+    rows_seq = n_rows // n_seq
     slots_seq = rows_seq // steps
+    halves = n_seq // n_own
+    width = n_seq * 128
 
     def seq_peer(s):
         return (tok, s, kv)
@@ -165,6 +177,12 @@
         part = buffer.at[pl.ds(0, count)]
         pltpu.make_async_copy(part, part, send_sem.at[index]).wait()
 
+    def pair_at(k):
+        dz = lax.rem(k // 2, 2) * 2 + k // 4
+        return lax.rem(seq // 4 + dz, n_seq // 4) * 2 + lax.rem(seq // 2 + k, 2)
+
+    near = [pair_at(jnp.int32(k)) for k in (0, 1, 4, 5, 6, 7, 2, 3)]
+
     sub8 = iota((8, 128), 0)
 
     def ids_block(b, carry):
@@ -175,11 +193,11 @@
         ids_v[pl.ds(pl.multiple_of(b * 8, 8), 8), :] = value
         return carry
 
-    lax.fori_loop(0, n_req * steps // 8, ids_block, 0)
+    lax.fori_loop(0, n_rows // 8, ids_block, 0)
+    gain2[...] = gain2_ref[...].astype(F32)
 
     table_load.wait()
     kt = 512
-    n_rows = n_req * steps
     wide_ids = jnp.concatenate([ids_v[...]] * (kt // 128), axis=1) - own * vocab
     lane_k = iota((n_rows, kt), 1)
 
@@ -200,22 +218,46 @@
     x_own = x_recv[0].astype(F32)
     for g in range(1, n_own):
         x_own = x_own + x_recv[g].astype(F32)
-
-    x_all[own] = x_own.astype(BF16)
-    for d in range(1, n_own):
-        g = lax.rem(own + d, n_own)
-        own_copy(1, x_all.at[own], x_all.at[own], g).start()
-    own_wait(1, x_all)
-
-    per = rows_own // rows_seq
-
-    def seq_rows(s):
-        return x_all.at[s // per, pl.ds(pl.multiple_of(lax.rem(s, per) * rows_seq, rows_seq), rows_seq)]
-
-    for d in range(1, n_seq):
-        s = lax.rem(seq + d, n_seq)
-        seq_copy(0, seq_rows(s), x_rows.at[seq], s).start()
-    x_rows[seq] = seq_rows(seq)[...]
+    x_own_v[...] = x_own.astype(BF16).reshape(halves, rows_seq, 128)
+
+    def x_copy(half, g):
+        s = own * halves + half
+        return pltpu.make_async_remote_copy(
+            src_ref=x_own_v.at[half],
+            dst_ref=x_rows.at[seq],
+            send_sem=send_sem.at[3],
+            recv_sem=seq_sem.at[0, seq],
+            device_id=(g // n_kv, s, lax.rem(g, n_kv)),
+            device_id_type=MESH,
+        )
+
+    holds_own = own == seq // halves
+    for half in range(halves):
+        for d in range(1, n_own):
+            x_copy(half, lax.rem(own + d, n_own)).start()
+
+        @pl.when(own * halves + half != seq)
+        def _():
+            x_copy(half, own).start()
+
+    @pl.when(holds_own)
+    def _():
+        x_rows[seq] = x_own_v[lax.rem(seq, halves)]
+
+    for c in cache_loads:
+        c.wait()
+
+    def pack(m, carry):
+        size = 256
+        low = iota((size, 128), 1) < 64
+        for t in range(ctx // size):
+            a = cache[order_ref[2 * m], t * size : (t + 1) * size, :]
+            b = cache[order_ref[2 * m + 1], t * size : (t + 1) * size, :]
+            keys[m, t * size : (t + 1) * size, :] = jnp.where(low, a, pltpu.roll(b, 64, 1))
+            vals[m, t * size : (t + 1) * size, :] = jnp.where(low, pltpu.roll(a, 64, 1), b)
+        return carry
+
+    lax.fori_loop(0, n_req // 2, pack, 0)
 
     row16 = iota((rows_seq, 128), 0)
     lane16 = iota((rows_seq, 128), 1)
@@ -237,78 +279,100 @@
         swapped = jnp.where(front, -pltpu.roll(v, 96, 1), pltpu.roll(v, 32, 1))
         return v * cosine + swapped * sine
 
-    seq_wait_all(0, x_rows)
-    width = n_seq * 128
+    gain = jnp.concatenate([gain_ref[s : s + 1, :].astype(F32) for s in range(n_seq)], axis=1)
+    wq_load.wait()
+    wkv_load.wait()
+
+    for s in range(n_seq):
+
+        @pl.when(jnp.logical_not(holds_own) | (seq != s))
+        def _():
+            seq_wait(0, x_rows, s)
+
     x16 = jnp.concatenate([x_rows[s] for s in range(n_seq)], axis=1).astype(F32)
     inv_attn = lax.rsqrt(jnp.sum(x16 * x16, axis=1, keepdims=True) / width + EPSILON)
-    scaled = (x16 * gain_ref[0:1, :]).astype(BF16)
-    wq_load.wait()
-    wkv_load.wait()
+    scaled = (x16 * gain).astype(BF16)
     q_raw = dot(scaled, wq[...]) * inv_attn
     kv_raw = dot(scaled, wkv[...]) * inv_attn
-    q_tiles = [rotate(q_raw[:, t * 128 : (t + 1) * 128]).astype(BF16) for t in range(2)]
-    low = lane16 < 64
-    fresh = jnp.where(low, rotate(kv_raw), kv_raw).astype(BF16).astype(F32)
-    q_all[seq] = jnp.concatenate(q_tiles, axis=1)
-    for d in range(1, n_seq):
-        s = lax.rem(seq + d, n_seq)
-        seq_copy(1, q_all.at[seq], q_all.at[seq], s).start()
-
-    key_lo = jnp.where(low, fresh, 0.0)
-    val_hi = jnp.where(low, 0.0, fresh)
-    keys = [key_lo.astype(BF16), pltpu.roll(key_lo, 64, 1).astype(BF16)]
-    values = [pltpu.roll(val_hi, 64, 1).astype(BF16), val_hi.astype(BF16)]
-    r_i = iota((rows_seq, rows_seq), 0)
-    c_i = iota((rows_seq, rows_seq), 1)
-    causal = (r_i // steps == c_i // steps) & (c_i <= r_i)
+    q_tiles = [rotate(q_raw[:, t * 128 : (t + 1) * 128]) for t in range(2)]
+    query = interleave(q_tiles, slots_seq, steps).astype(BF16)
+    q_all[seq] = query
+    for k in (6, 7, 2, 3, 4, 5, 1, 0):
+        for a in range(2):
+            s = near[k] * 2 + a
+            if k:
+                seq_copy(1, q_all.at[seq], q_all.at[seq], s).start()
+            else:
+
+                @pl.when(s != seq)
+                def _():
+                    seq_copy(1, q_all.at[seq], q_all.at[seq], s).start()
+
+    rows_q = 2 * rows_seq
+    low16 = lane16 < 64
+    low32 = iota((rows_q, 128), 1) < 64
+    fresh = jnp.where(low16, rotate(kv_raw), kv_raw).astype(BF16).astype(F32)
+    key_lo = jnp.where(low16, fresh, 0.0)
+    val_hi = jnp.where(low16, 0.0, fresh)
+    f_keys = [key_lo.astype(BF16), pltpu.roll(key_lo, 64, 1).astype(BF16)]
+    f_vals = [pltpu.roll(val_hi, 64, 1).astype(BF16), val_hi.astype(BF16)]
+    r_i = iota((rows_q, rows_seq), 0)
+    c_i = iota((rows_q, rows_seq), 1)
+    causal = (r_i // (2 * steps) == c_i // steps) & (lax.rem(c_i, steps) <= lax.rem(r_i, steps))
     f_peak, f_mass, f_acc = [], [], []
-    for h in range(4):
-        t = jnp.where(causal, dot_nt(q_tiles[h // 2], keys[h % 2]) * 0.125, FLOOR_SCORE)
+    for hb in range(2):
+        t = jnp.where(causal, dot_nt(query, f_keys[hb]) * 0.125, FLOOR_SCORE)
         peak = jnp.max(t, axis=1, keepdims=True)
         w = jnp.where(causal, jnp.exp(t - peak), 0.0).astype(BF16)
         f_peak.append(peak)
         f_mass.append(jnp.sum(w.astype(F32), axis=1, keepdims=True))
-        f_acc.append(dot(w, values[h % 2]))
-
-    for c in cache_loads:
-        c.wait()
-    seq_wait_all(1, q_all)
+        f_acc.append(dot(w, f_vals[hb]))
 
     group = 8
     n_group = n_req // group
-    pt = 256
-    lane_slot = lax.rem(iota((1, 128), 1), group * steps) // steps
-    row_slot = lax.rem(iota((128, 128), 0), group * steps) // steps
-    lane32 = iota((group * steps, 128), 1)
-    value_slot = lax.rem(iota((128, 256), 0), group * steps) // steps
+    pt = 512
+    lane_slot = iota((1, 128), 1) // 16
+    low8 = iota((8, 128), 1) < 64
 
     def attend(k, carry):
-        grp = lax.rem(seq // 2 + 1 + k, n_group)
-        q32 = q_all[pl.ds(grp * 2, 2)].reshape(group * steps, 256).astype(F32)
-        pieces = []
-        for h in range(4):
-            tile = q32[:, (h // 2) * 128 : (h // 2 + 1) * 128]
-            if h % 2:
-                tile = pltpu.roll(tile, 64, 1)
-            pieces.append(jnp.where(lane32 < 64, tile, 0.0))
-        q128 = jnp.concatenate(pieces, axis=0) * 0.125
-        requests = [order_ref[grp * group + r] for r in range(group)]
+        grp = pair_at(k)
+        for a in range(2):
+            s = grp * 2 + a
+
+            @pl.when(s != seq)
+            def _():
+                seq_wait(1, q_all, s)
+
+        q64 = q_all[pl.ds(grp * 2, 2)].reshape(2 * rows_q, 128).astype(F32) * 0.125
+        r64 = pltpu.roll(q64, 64, 1)
+        zero = jnp.zeros((32, 128), F32)
+        columns = []
+        for m in range(group // 2):
+            e, o = slice(16 * m, 16 * m + 8), slice(16 * m + 8, 16 * m + 16)
+            block = jnp.concatenate(
+                [
+                    jnp.where(low8, q64[e], 0.0),
+                    jnp.where(low8, r64[e], 0.0),
+                    jnp.where(low8, 0.0, r64[o]),
+                    jnp.where(low8, 0.0, q64[o]),
+                ],
+                axis=0,
+            )
+            columns.append(
+                jnp.concatenate([block if i == m else zero for i in range(group // 2)], axis=0)
+            )
+        rhs = jnp.concatenate(columns, axis=1).astype(BF16)
         lengths = jnp.zeros((1, 128), jnp.int32)
         for r in range(group):
-            lengths = jnp.where(lane_slot == r, len_ref[requests[r]], lengths)
+            lengths = jnp.where(lane_slot == r, len_ref[order_ref[grp * group + r]], lengths)
         lengths = lengths - seq * ctx
-        rhs = jnp.concatenate(
-            [jnp.where(row_slot == r, q128, 0.0).astype(BF16) for r in range(group)], axis=1
-        )
-        q_rows[...] = rhs
         peak = jnp.full((1, 128), FLOOR_SCORE, F32)
         for t in range(ctx // pt):
             lhs = jnp.concatenate(
-                [cache[requests[r], t * pt : (t + 1) * pt, :] for r in range(group)], axis=1
+                [keys[grp * 4 + m, t * pt : (t + 1) * pt, :] for m in range(group // 2)], axis=1
             )
-            scores = dot_nt(lhs, q_rows[...])
             live = iota((pt, 128), 0) + t * pt < lengths
-            scores = jnp.where(live, scores, FLOOR_SCORE)
+            scores = jnp.where(live, dot_nt(lhs, rhs), FLOOR_SCORE)
             s_scr[t * pt : (t + 1) * pt, :] = scores
             peak = jnp.maximum(peak, jnp.max(scores, axis=0, keepdims=True))
         mass = jnp.zeros((1, 128), F32)
@@ -318,27 +382,24 @@
             w = jnp.where(live, w, 0.0).astype(BF16)
             mass = mass + jnp.sum(w.astype(F32), axis=0, keepdims=True)
             p_scr[:, t * pt : (t + 1) * pt] = w.T
-        total = jnp.zeros((128, 128), F32)
-        for r in range(0, group, 2):
-            both = jnp.concatenate([cache[requests[r]], cache[requests[r + 1]]], axis=1)
-            both = dot(p_scr[...], both)
-            total = jnp.where(row_slot == r, both[:, :128], total)
-            total = jnp.where(row_slot == r + 1, both[:, 128:], total)
         st_send[grp] = jnp.concatenate([peak, mass], axis=0)
-        for pair in range(2):
-            even = pltpu.roll(total[pair * 64 : pair * 64 + 32], 64, 1)
-            tile = jnp.where(lane32 < 64, even, total[pair * 64 + 32 : pair * 64 + 64])
-            for a in range(2):
-                acc_send[grp * 2 + a, pair * rows_seq : (pair + 1) * rows_seq] = tile[
-                    a * rows_seq : (a + 1) * rows_seq
-                ].astype(BF16)
         for a in range(2):
+            both = jnp.concatenate([vals[grp * 4 + 2 * a], vals[grp * 4 + 2 * a + 1]], axis=1)
+            total = dot(p_scr[a * 64 : (a + 1) * 64, :], both)
+            pieces = []
+            for i in range(slots_seq):
+                tile = total[16 * i : 16 * i + 16, (i // 2) * 128 : (i // 2 + 1) * 128]
+                if i % 2:
+                    pieces.append(jnp.where(low8, pltpu.roll(tile[:8], 64, 1), tile[8:]))
+                else:
+                    pieces.append(jnp.where(low8, tile[:8], pltpu.roll(tile[8:], 64, 1)))
             s = grp * 2 + a
+            acc_send[s] = jnp.concatenate(pieces, axis=0).astype(BF16)
 
             @pl.when(s != seq)
             def _():
+                seq_copy(3, st_send.at[grp], st_recv.at[seq], s).start()
                 seq_copy(2, acc_send.at[s], acc_recv.at[seq], s).start()
-                seq_copy(3, st_send.at[grp], st_recv.at[seq], s).start()
 
         return carry
 
@@ -349,31 +410,42 @@
     seq_wait_all(3, st_recv)
     stats = jnp.concatenate([st_recv[:, 0, :], st_recv[:, 1, :]], axis=0)
     st_t[...] = jnp.concatenate([stats, jnp.zeros((128 - 2 * n_seq, 128), F32)], axis=0).T
+    mine = st_t[pl.ds(pl.multiple_of(lax.rem(seq, 2) * 64, 64), 64), :]
     shares, f_share = [], []
-    for h in range(4):
-        offset = pl.multiple_of(h * 32 + lax.rem(seq, 2) * rows_seq, rows_seq)
-        block = st_t[pl.ds(offset, rows_seq), :]
+    for hb in range(2):
+        block = jnp.concatenate(
+            [mine[16 * i + 8 * hb : 16 * i + 8 * hb + 8] for i in range(slots_seq)], axis=0
+        )
         peaks, masses = block[:, :n_seq], block[:, n_seq : 2 * n_seq]
-        top = jnp.maximum(jnp.max(peaks, axis=1, keepdims=True), f_peak[h])
+        top = jnp.maximum(jnp.max(peaks, axis=1, keepdims=True), f_peak[hb])
         factor = jnp.exp(peaks - top)
-        f_factor = jnp.exp(f_peak[h] - top)
-        denom = jnp.sum(factor * masses, axis=1, keepdims=True) + f_factor * f_mass[h]
+        f_factor = jnp.exp(f_peak[hb] - top)
+        denom = jnp.sum(factor * masses, axis=1, keepdims=True) + f_factor * f_mass[hb]
         shares.append(factor / denom)
         f_share.append(f_factor / denom)
-    tiles = []
-    for pair in range(2):
-        tiles.append(f_acc[2 * pair] * f_share[2 * pair] + f_acc[2 * pair + 1] * f_share[2 * pair + 1])
+    weights = [jnp.where(low32, shares[0][:, s : s + 1], shares[1][:, s : s + 1]) for s in range(n_seq)]
+    attended = f_acc[0] * f_share[0] + f_acc[1] * f_share[1]
     seq_wait_all(2, acc_recv)
     for s in range(n_seq):
-        part = acc_recv[s].astype(F32)
-        for pair in range(2):
-            weight = jnp.where(low, shares[2 * pair][:, s : s + 1], shares[2 * pair + 1][:, s : s + 1])
-            tiles[pair] = tiles[pair] + weight * part[pair * rows_seq : (pair + 1) * rows_seq]
-
-    at_all[seq] = jnp.concatenate([t.astype(BF16) for t in tiles], axis=1)
-    for d in range(1, n_seq):
-        s = lax.rem(seq + d, n_seq)
-        seq_copy(4, at_all.at[seq], at_all.at[seq], s).start()
+        attended = attended + weights[s] * acc_recv[s].astype(F32)
+
+    at_rows = [
+        jnp.concatenate(
+            [attended[8 * i + 4 * t : 8 * i + 4 * t + 4] for i in range(slots_seq)], axis=0
+        )
+        for t in range(2)
+    ]
+    at_all[seq] = jnp.concatenate(at_rows, axis=1).astype(BF16)
+    for k in (6, 7, 2, 3, 4, 5, 1, 0):
+        for a in range(2):
+            s = near[k] * 2 + a
+            if k:
+                seq_copy(4, at_all.at[seq], at_all.at[seq], s).start()
+            else:
+
+                @pl.when(s != seq)
+                def _():
+                    seq_copy(4, at_all.at[seq], at_all.at[seq], s).start()
     wo_load.wait()
     seq_wait_all(4, at_all)
     partial = dot(at_all[...].reshape(n_rows, 256), wo[...]).astype(BF16)
@@ -388,26 +460,61 @@
         attn = attn + o_recv[g].astype(F32)
     mid = (x_own + attn).astype(BF16)
     mid_all[seq] = mid
-    for d in range(1, n_seq):
-        s = lax.rem(seq + d, n_seq)
-        seq_copy(5, mid_all.at[seq], mid_all.at[seq], s).start()
+    for k in (6, 7, 2, 3, 4, 5, 1, 0):
+        for a in range(2):
+            s = near[k] * 2 + a
+            if k:
+                seq_copy(5, mid_all.at[seq], mid_all.at[seq], s).start()
+            else:
+
+                @pl.when(s != seq)
+                def _():
+                    seq_copy(5, mid_all.at[seq], mid_all.at[seq], s).start()
 
     wg_load.wait()
     wu_load.wait()
-    seq_wait_all(5, mid_all)
-    m = jnp.concatenate([mid_all[s] for s in range(n_seq)], axis=1).astype(F32)
-    inv_mlp = lax.rsqrt(jnp.sum(m * m, axis=1, keepdims=True) / width + EPSILON)
-    scaled_mid = (m * gain_ref[1:2, :]).astype(BF16)
-    gate = dot(scaled_mid, wg[...]) * inv_mlp
-    up = dot(scaled_mid, wu[...]) * inv_mlp
-    hidden = (gate / (1.0 + jnp.exp(-gate)) * up).astype(BF16)
     wd_load.wait()
-    down = dot(hidden, wd[...]).astype(BF16)
-    for s in range(n_seq):
-        d_send[s] = down[:, s * 128 : (s + 1) * 128]
-    for d in range(1, n_seq):
-        s = lax.rem(seq + d, n_seq)
-        seq_copy(6, d_send.at[s], d_recv.at[seq], s).start()
+    ff = wg.shape[1]
+    gate = jnp.zeros((rows_own, ff), F32)
+    up = jnp.zeros((rows_own, ff), F32)
+    squares = jnp.zeros((rows_own, 128), F32)
+    for k in range(n_seq // 2):
+        pair = near[k]
+        parts = []
+        for a in range(2):
+            s = pair * 2 + a
+            if k:
+                seq_wait(5, mid_all, s)
+            else:
+
+                @pl.when(s != seq)
+                def _():
+                    seq_wait(5, mid_all, s)
+
+            m = mid_all[s].astype(F32)
+            squares = squares + m * m
+            parts.append((m * gain2[pl.ds(s, 1), :]).astype(BF16))
+        both = jnp.concatenate(parts, axis=1)
+        rows = pl.ds(pl.multiple_of(pair * 256, 256), 256)
+        gate = gate + dot(both, wg[rows, :])
+        up = up + dot(both, wu[rows, :])
+    inv_mlp = lax.rsqrt(jnp.sum(squares, axis=1, keepdims=True) / width + EPSILON)
+    gate = gate * inv_mlp
+    hidden = (gate / (1.0 + jnp.exp(-gate)) * (up * inv_mlp)).astype(BF16)
+    for k in (6, 7, 2, 3, 4, 5, 1, 0):
+        pair = near[k]
+        down = dot(hidden, wd[:, pl.ds(pl.multiple_of(pair * 256, 256), 256)]).astype(BF16)
+        for a in range(2):
+            s = pair * 2 + a
+            d_send[s] = down[:, a * 128 : (a + 1) * 128]
+            if k:
+                seq_copy(6, d_send.at[s], d_recv.at[seq], s).start()
+            else:
+
+                @pl.when(s != seq)
+                def _():
+                    seq_copy(6, d_send.at[s], d_recv.at[seq], s).start()
+
     d_recv[seq] = d_send[seq]
     seq_wait_all(6, d_recv)
     result = mid.astype(F32)
@@ -416,9 +523,13 @@
     out_ref[...] = result.astype(BF16).reshape(out_ref.shape)
 
     sent(0, x_recv, n_own - 1)
-    sent(1, x_all, n_own - 1)
     sent(2, o_recv, n_own - 1)
     sent(3, x_rows, n_seq - 1)
+
+    @pl.when(jnp.logical_not(holds_own))
+    def _():
+        sent(3, x_rows, 1)
+
     sent(4, q_all, n_seq - 1)
     sent(5, acc_recv, n_seq - 1)
     sent(6, st_recv, n_seq - 1)
@@ -453,7 +564,6 @@
         rows = n_req * steps
         r_own, r_seq = rows // n_own, rows // n_seq
         width = proj_query.shape[0]
-        gains = jnp.stack([attn_gain, mlp_gain]).astype(F32)
         smem = pl.BlockSpec(memory_space=pltpu.SMEM)
         vmem = pl.BlockSpec(memory_space=pltpu.VMEM)
         hbm = pl.BlockSpec(memory_space=pl.ANY)
@@ -469,13 +579,15 @@
         ]
         scratch = [pltpu.VMEM(w.shape, w.dtype) for w in weights]
         scratch += [
+            pltpu.VMEM((n_req // 2, ctx, 128), BF16),
+            pltpu.VMEM((n_req // 2, ctx, 128), BF16),
+            pltpu.VMEM((n_seq, 128), F32),
             pltpu.VMEM((rows, 128), jnp.int32),
             pltpu.VMEM((n_own, r_own, 128), BF16),
             pltpu.VMEM((n_own, r_own, 128), BF16),
-            pltpu.VMEM((n_own, r_own, 128), BF16),
+            pltpu.VMEM((n_seq // n_own, r_seq, 128), BF16),
             pltpu.VMEM((n_seq, r_seq, 128), BF16),
-            pltpu.VMEM((n_seq, r_seq, 256), BF16),
-            pltpu.VMEM((128, 1024), BF16),
+            pltpu.VMEM((n_seq, 2 * r_seq, 128), BF16),
             pltpu.VMEM((ctx, 128), F32),
             pltpu.VMEM((128, ctx), BF16),
             pltpu.VMEM((n_seq, 2 * r_seq, 128), BF16),
@@ -497,14 +609,22 @@
         return pl.pallas_call(
             functools.partial(layer_kernel, n_tok, n_seq, n_kv),
             out_shape=jax.ShapeDtypeStruct((n_req // n_own, steps, 128), BF16),
-            in_specs=[smem, smem, smem, vmem, vmem] + [hbm] * len(weights),
+            in_specs=[smem, smem, smem, vmem, vmem, vmem] + [hbm] * len(weights),
             out_specs=vmem,
             scratch_shapes=scratch,
             compiler_params=pltpu.CompilerParams(
                 collective_id=0, has_side_effects=True, vmem_limit_bytes=64 * 1000 * 1000
             ),
             name="layer",
-        )(token_ids.T, request_order, cache_lengths, gains, jnp.asarray(freq), *weights)
+        )(
+            token_ids.T,
+            request_order,
+            cache_lengths,
+            attn_gain.reshape(n_seq, 128),
+            mlp_gain.reshape(n_seq, 128),
+            jnp.asarray(freq),
+            *weights,
+        )
 
     placed = (
         P(),

time: 67.4 us -> 61 us (0.905)
  Pallas kernels: 63.9 us -> 59.5 us
  local copies, waits for them, and re-layouts: 2.69 us -> 1.3 us
    pallas_call x1, Pallas kernels: 63.9 us -> 59.5 us  [per_device(): pl.pallas_call(functools.partial(layer_kernel, n_tok, n_seq, n_kv), out_s...]
    another operation x2 -> x0, local copies, waits for them, and re-layouts: 1.39 us -> none  [per_device(): gains = jnp.stack([attn_gain, mlp_gain]).astype(F32)]
where the time goes in v2:
time: 61 us; the launch traced here: 60.8 us
  Pallas kernels  59.5 us (98%)
  local copies, waits for them, and re-layouts  1.3 us (2%)
    pallas_call x1, Pallas kernels, per_device(): pl.pallas_call(functools.partial(layer_kernel, n_tok, n_seq, n_kv), out_s...  59.5 us
    unnamed x1, local copies, waits for them, and re-layouts  1.3 us

profile of v2, /device:TPU:0, one launch (start us, length us, event | category | flops | bytes accessed | tf_op | source)
XLA Modules:
  0.0 60.8 jit_solution(11724257778121775628)
XLA Ops:
  0.0 59.5 %layer.1 = bf16[8,4,128]{2,1,0:T(4,128)(2,1)} custom-call(s32[4,64]{1,0:T(4,128)} %bitcast.9, s32[64]{0:T(128)} %order_ref.1, s32[64]{0:T(128)} %len_ref.1, bf16[16,128]{1,0:T(8,128)(2,1)} %bitcast.7, bf16[16,128]{1,0:T(8,128)(2,1)} %bitcast.8, f32[1,128]{1,0:T(1,128)} %constant.2.clone.freq_ref, bf16[4096,128]{1,0:T(8,128)(2,1)} %table_hbm.1, ...), custom_call_target="tpu_custom_call" | custom-call | tf_op jit(solution)/shard_map/layer/pallas_call | solution.py:609
  59.5 1.3 %copy.16 = bf16[8,4,128]{2,1,0:T(4,128)(2,1)} copy(bf16[8,4,128]{2,1,0:T(4,128)(2,1)} %layer.1) | data formatting | bytes 16384

commit v3 on v2

--- a/solution.py
+++ b/solution.py
@@ -62,7 +62,6 @@
     wu,
     wd,
     keys,
-    vals,
     gain2,
     ids_v,
     x_send,
@@ -70,8 +69,10 @@
     x_own_v,
     x_rows,
     q_all,
-    s_scr,
-    p_scr,
+    s_even,
+    s_odd,
+    p_even,
+    p_odd,
     acc_send,
     acc_recv,
     st_send,
@@ -254,7 +255,6 @@
             a = cache[order_ref[2 * m], t * size : (t + 1) * size, :]
             b = cache[order_ref[2 * m + 1], t * size : (t + 1) * size, :]
             keys[m, t * size : (t + 1) * size, :] = jnp.where(low, a, pltpu.roll(b, 64, 1))
-            vals[m, t * size : (t + 1) * size, :] = jnp.where(low, pltpu.roll(a, 64, 1), b)
         return carry
 
     lax.fori_loop(0, n_req // 2, pack, 0)
@@ -334,15 +334,16 @@
     lane_slot = iota((1, 128), 1) // 16
     low8 = iota((8, 128), 1) < 64
 
-    def attend(k, carry):
-        grp = pair_at(k)
+    def arrive(k):
         for a in range(2):
-            s = grp * 2 + a
+            s = pair_at(k) * 2 + a
 
             @pl.when(s != seq)
             def _():
                 seq_wait(1, q_all, s)
 
+    def score(k, s_scr):
+        grp = pair_at(k)
         q64 = q_all[pl.ds(grp * 2, 2)].reshape(2 * rows_q, 128).astype(F32) * 0.125
         r64 = pltpu.roll(q64, 64, 1)
         zero = jnp.zeros((32, 128), F32)
@@ -375,35 +376,60 @@
             scores = jnp.where(live, dot_nt(lhs, rhs), FLOOR_SCORE)
             s_scr[t * pt : (t + 1) * pt, :] = scores
             peak = jnp.maximum(peak, jnp.max(scores, axis=0, keepdims=True))
+        return peak, lengths
+
+    def weigh(k, s_scr, p_scr, peak, lengths):
+        grp = pair_at(k)
+        shift = jnp.where(lengths > 0, peak, 0.0)
         mass = jnp.zeros((1, 128), F32)
         for t in range(ctx // pt):
-            live = iota((pt, 128), 0) + t * pt < lengths
-            w = jnp.exp(s_scr[t * pt : (t + 1) * pt, :] - peak)
-            w = jnp.where(live, w, 0.0).astype(BF16)
+            w = jnp.exp(s_scr[t * pt : (t + 1) * pt, :] - shift).astype(BF16)
             mass = mass + jnp.sum(w.astype(F32), axis=0, keepdims=True)
             p_scr[:, t * pt : (t + 1) * pt] = w.T
         st_send[grp] = jnp.concatenate([peak, mass], axis=0)
         for a in range(2):
-            both = jnp.concatenate([vals[grp * 4 + 2 * a], vals[grp * 4 + 2 * a + 1]], axis=1)
-            total = dot(p_scr[a * 64 : (a + 1) * 64, :], both)
             pieces = []
-            for i in range(slots_seq):
-                tile = total[16 * i : 16 * i + 16, (i // 2) * 128 : (i // 2 + 1) * 128]
-                if i % 2:
+            for i in range(0, slots_seq, 2):
+                r = a * slots_seq + i
+                both = jnp.concatenate(
+                    [cache[order_ref[grp * group + r + e]] for e in range(2)], axis=1
+                )
+                total = dot(p_scr[r * 16 : r * 16 + 32, :], both)
+                for e in range(2):
+                    tile = total[16 * e : 16 * e + 16, e * 128 : e * 128 + 128]
                     pieces.append(jnp.where(low8, pltpu.roll(tile[:8], 64, 1), tile[8:]))
-                else:
-                    pieces.append(jnp.where(low8, tile[:8], pltpu.roll(tile[8:], 64, 1)))
+            acc_send[grp * 2 + a] = jnp.concatenate(pieces, axis=0).astype(BF16)
+
+    def deliver(k):
+        grp = pair_at(k)
+        for a in range(2):
             s = grp * 2 + a
-            acc_send[s] = jnp.concatenate(pieces, axis=0).astype(BF16)
 
             @pl.when(s != seq)
             def _():
                 seq_copy(3, st_send.at[grp], st_recv.at[seq], s).start()
                 seq_copy(2, acc_send.at[s], acc_recv.at[seq], s).start()
 
+    def attend(i, carry):
+        arrive(2 * i + 1)
+        following = score(2 * i + 1, s_odd)
+        weigh(2 * i, s_even, p_even, *carry)
+        deliver(2 * i)
+        arrive(2 * i + 2)
+        carry = score(2 * i + 2, s_even)
+        weigh(2 * i + 1, s_odd, p_odd, *following)
+        deliver(2 * i + 1)
         return carry
 
-    lax.fori_loop(0, n_group, attend, 0)
+    arrive(jnp.int32(0))
+    carry = lax.fori_loop(0, n_group // 2 - 1, attend, score(jnp.int32(0), s_even))
+    last = jnp.int32(n_group - 2)
+    arrive(last + 1)
+    following = score(last + 1, s_odd)
+    weigh(last, s_even, p_even, *carry)
+    deliver(last)
+    weigh(last + 1, s_odd, p_odd, *following)
+    deliver(last + 1)
 
     acc_recv[seq] = acc_send[seq]
     st_recv[seq] = st_send[seq // 2]
@@ -501,19 +527,20 @@
     inv_mlp = lax.rsqrt(jnp.sum(squares, axis=1, keepdims=True) / width + EPSILON)
     gate = gate * inv_mlp
     hidden = (gate / (1.0 + jnp.exp(-gate)) * (up * inv_mlp)).astype(BF16)
-    for k in (6, 7, 2, 3, 4, 5, 1, 0):
-        pair = near[k]
-        down = dot(hidden, wd[:, pl.ds(pl.multiple_of(pair * 256, 256), 256)]).astype(BF16)
-        for a in range(2):
-            s = pair * 2 + a
-            d_send[s] = down[:, a * 128 : (a + 1) * 128]
-            if k:
-                seq_copy(6, d_send.at[s], d_recv.at[seq], s).start()
-            else:
-
-                @pl.when(s != seq)
-                def _():
+    for ks in ((6, 7, 2, 3), (4, 5, 1, 0)):
+        columns = [wd[:, pl.ds(pl.multiple_of(near[k] * 256, 256), 256)] for k in ks]
+        down = dot(hidden, jnp.concatenate(columns, axis=1)).astype(BF16)
+        for n, k in enumerate(ks):
+            for a in range(2):
+                s = near[k] * 2 + a
+                d_send[s] = down[:, n * 256 + a * 128 : n * 256 + (a + 1) * 128]
+                if k:
                     seq_copy(6, d_send.at[s], d_recv.at[seq], s).start()
+                else:
+
+                    @pl.when(s != seq)
+                    def _():
+                        seq_copy(6, d_send.at[s], d_recv.at[seq], s).start()
 
     d_recv[seq] = d_send[seq]
     seq_wait_all(6, d_recv)
@@ -580,7 +607,6 @@
         scratch = [pltpu.VMEM(w.shape, w.dtype) for w in weights]
         scratch += [
             pltpu.VMEM((n_req // 2, ctx, 128), BF16),
-            pltpu.VMEM((n_req // 2, ctx, 128), BF16),
             pltpu.VMEM((n_seq, 128), F32),
             pltpu.VMEM((rows, 128), jnp.int32),
             pltpu.VMEM((n_own, r_own, 128), BF16),
@@ -589,6 +615,8 @@
             pltpu.VMEM((n_seq, r_seq, 128), BF16),
             pltpu.VMEM((n_seq, 2 * r_seq, 128), BF16),
             pltpu.VMEM((ctx, 128), F32),
+            pltpu.VMEM((ctx, 128), F32),
+            pltpu.VMEM((128, ctx), BF16),
             pltpu.VMEM((128, ctx), BF16),
             pltpu.VMEM((n_seq, 2 * r_seq, 128), BF16),
             pltpu.VMEM((n_seq, 2 * r_seq, 128), BF16),

time: 61 us -> 57.8 us (0.948)
  Pallas kernels: 59.5 us -> 56.3 us
    pallas_call x1, Pallas kernels: 59.5 us -> 56.3 us  [per_device(): pl.pallas_call(functools.partial(layer_kernel, n_tok, n_seq, n_kv), out_s...]
where the time goes in v3:
time: 57.8 us; the launch traced here: 57.6 us
  Pallas kernels  56.3 us (97%)
  local copies, waits for them, and re-layouts  1.3 us (2%)
    pallas_call x1, Pallas kernels, per_device(): pl.pallas_call(functools.partial(layer_kernel, n_tok, n_seq, n_kv), out_s...  56.3 us
    unnamed x1, local copies, waits for them, and re-layouts  1.3 us

profile of v3, /device:TPU:0, one launch (start us, length us, event | category | flops | bytes accessed | tf_op | source)
XLA Modules:
  0.0 57.6 jit_solution(5364295267971325829)
XLA Ops:
  0.0 56.3 %layer.1 = bf16[8,4,128]{2,1,0:T(4,128)(2,1)} custom-call(s32[4,64]{1,0:T(4,128)} %bitcast.9, s32[64]{0:T(128)} %order_ref.1, s32[64]{0:T(128)} %len_ref.1, bf16[16,128]{1,0:T(8,128)(2,1)} %bitcast.7, bf16[16,128]{1,0:T(8,128)(2,1)} %bitcast.8, f32[1,128]{1,0:T(1,128)} %constant.2.clone.freq_ref, bf16[4096,128]{1,0:T(8,128)(2,1)} %table_hbm.1, ...), custom_call_target="tpu_custom_call" | custom-call | tf_op jit(solution)/shard_map/layer/pallas_call | solution.py:637
  56.3 1.3 %copy.16 = bf16[8,4,128]{2,1,0:T(4,128)(2,1)} copy(bf16[8,4,128]{2,1,0:T(4,128)(2,1)} %layer.1) | data formatting | bytes 16384

commit v4 on v3

--- a/solution.py
+++ b/solution.py
@@ -38,12 +38,12 @@
     n_tok,
     n_seq,
     n_kv,
-    ids_ref,
-    order_ref,
-    len_ref,
-    gain_ref,
-    gain2_ref,
-    freq_ref,
+    ids_hbm,
+    order_hbm,
+    len_hbm,
+    gain_hbm,
+    gain2_hbm,
+    freq_hbm,
     table_hbm,
     wq_hbm,
     wkv_hbm,
@@ -53,6 +53,12 @@
     wu_hbm,
     wd_hbm,
     out_ref,
+    ids_ref,
+    order_ref,
+    len_ref,
+    gain_ref,
+    gain2_ref,
+    freq_ref,
     table,
     wq,
     wkv,
@@ -111,6 +117,16 @@
     def own_peer(g):
         return (g // n_kv, seq, lax.rem(g, n_kv))
 
+    loads = []
+
+    def load(src, dst):
+        copy = pltpu.make_async_copy(src, dst, load_sem.at[len(loads)])
+        copy.start()
+        loads.append(copy)
+        return copy
+
+    table_load = load(table_hbm, table)
+    small_loads = [load(ids_hbm, ids_ref), load(order_hbm, order_ref), load(len_hbm, len_ref)]
     barrier = pltpu.get_barrier_semaphore()
     for d in range(1, n_own):
         pl.semaphore_signal(
@@ -120,16 +136,7 @@
         pl.semaphore_signal(
             barrier, inc=1, device_id=seq_peer(lax.rem(seq + d, n_seq)), device_id_type=MESH
         )
-
-    loads = []
-
-    def load(src, dst):
-        copy = pltpu.make_async_copy(src, dst, load_sem.at[len(loads)])
-        copy.start()
-        loads.append(copy)
-        return copy
-
-    table_load = load(table_hbm, table)
+    gain_loads = [load(gain_hbm, gain_ref), load(gain2_hbm, gain2_ref), load(freq_hbm, freq_ref)]
     wq_load = load(wq_hbm, wq)
     wkv_load = load(wkv_hbm, wkv)
     chunk = 8
@@ -162,9 +169,13 @@
             device_id_type=MESH,
         )
 
+    owners = [
+        lax.rem(tok + dt, n_tok) * n_kv + lax.rem(kv + dk, n_kv)
+        for dt, dk in ((2, 0), (2, 1), (1, 0), (1, 1), (3, 0), (3, 1), (0, 1))
+    ]
+
     def own_wait(phase, dst):
-        for d in range(1, n_own):
-            g = lax.rem(own + d, n_own)
+        for g in owners:
             pltpu.make_async_copy(dst.at[g], dst.at[g], yc_sem.at[phase, g]).wait()
 
     def seq_wait(phase, dst, s):
@@ -179,10 +190,11 @@
         pltpu.make_async_copy(part, part, send_sem.at[index]).wait()
 
     def pair_at(k):
-        dz = lax.rem(k // 2, 2) * 2 + k // 4
-        return lax.rem(seq // 4 + dz, n_seq // 4) * 2 + lax.rem(seq // 2 + k, 2)
-
-    near = [pair_at(jnp.int32(k)) for k in (0, 1, 4, 5, 6, 7, 2, 3)]
+        dz = lax.rem(k + k // 4, 4)
+        return lax.rem(seq // 4 + dz, n_seq // 4) * 2 + lax.rem(seq // 2 + k // 4, 2)
+
+    near = [pair_at(jnp.int32(k)) for k in (0, 7, 1, 3, 4, 6, 2, 5)]
+    far = (7, 6, 5, 4, 3, 2, 1, 0)
 
     sub8 = iota((8, 128), 0)
 
@@ -194,8 +206,9 @@
         ids_v[pl.ds(pl.multiple_of(b * 8, 8), 8), :] = value
         return carry
 
+    for c in small_loads:
+        c.wait()
     lax.fori_loop(0, n_rows // 8, ids_block, 0)
-    gain2[...] = gain2_ref[...].astype(F32)
 
     table_load.wait()
     kt = 512
@@ -211,8 +224,7 @@
 
     pl.semaphore_wait(barrier, n_own - 1 + n_seq - 1)
 
-    for d in range(1, n_own):
-        g = lax.rem(own + d, n_own)
+    for g in owners:
         own_copy(0, x_send.at[g], x_recv.at[own], g).start()
     x_recv[own] = x_send[own]
     own_wait(0, x_recv)
@@ -258,6 +270,10 @@
         return carry
 
     lax.fori_loop(0, n_req // 2, pack, 0)
+
+    for c in gain_loads:
+        c.wait()
+    gain2[...] = gain2_ref[...].astype(F32)
 
     row16 = iota((rows_seq, 128), 0)
     lane16 = iota((rows_seq, 128), 1)
@@ -297,7 +313,7 @@
     q_tiles = [rotate(q_raw[:, t * 128 : (t + 1) * 128]) for t in range(2)]
     query = interleave(q_tiles, slots_seq, steps).astype(BF16)
     q_all[seq] = query
-    for k in (6, 7, 2, 3, 4, 5, 1, 0):
+    for k in far:
         for a in range(2):
             s = near[k] * 2 + a
             if k:
@@ -462,7 +478,7 @@
         for t in range(2)
     ]
     at_all[seq] = jnp.concatenate(at_rows, axis=1).astype(BF16)
-    for k in (6, 7, 2, 3, 4, 5, 1, 0):
+    for k in far:
         for a in range(2):
             s = near[k] * 2 + a
             if k:
@@ -476,8 +492,7 @@
     seq_wait_all(4, at_all)
     partial = dot(at_all[...].reshape(n_rows, 256), wo[...]).astype(BF16)
     o_send[...] = partial.reshape(n_own, rows_own, 128)
-    for d in range(1, n_own):
-        g = lax.rem(own + d, n_own)
+    for g in owners:
         own_copy(2, o_send.at[g], o_recv.at[own], g).start()
     o_recv[own] = o_send[own]
     own_wait(2, o_recv)
@@ -486,7 +501,7 @@
         attn = attn + o_recv[g].astype(F32)
     mid = (x_own + attn).astype(BF16)
     mid_all[seq] = mid
-    for k in (6, 7, 2, 3, 4, 5, 1, 0):
+    for k in far:
         for a in range(2):
             s = near[k] * 2 + a
             if k:
@@ -527,7 +542,7 @@
     inv_mlp = lax.rsqrt(jnp.sum(squares, axis=1, keepdims=True) / width + EPSILON)
     gate = gate * inv_mlp
     hidden = (gate / (1.0 + jnp.exp(-gate)) * (up * inv_mlp)).astype(BF16)
-    for ks in ((6, 7, 2, 3), (4, 5, 1, 0)):
+    for ks in (far[:4], far[4:]):
         columns = [wd[:, pl.ds(pl.multiple_of(near[k] * 256, 256), 256)] for k in ks]
         down = dot(hidden, jnp.concatenate(columns, axis=1)).astype(BF16)
         for n, k in enumerate(ks):
@@ -591,7 +606,6 @@
         rows = n_req * steps
         r_own, r_seq = rows // n_own, rows // n_seq
         width = proj_query.shape[0]
-        smem = pl.BlockSpec(memory_space=pltpu.SMEM)
         vmem = pl.BlockSpec(memory_space=pltpu.VMEM)
         hbm = pl.BlockSpec(memory_space=pl.ANY)
         weights = [
@@ -604,7 +618,15 @@
             proj_up,
             proj_down,
         ]
-        scratch = [pltpu.VMEM(w.shape, w.dtype) for w in weights]
+        scratch = [
+            pltpu.SMEM((steps, n_req), jnp.int32),
+            pltpu.SMEM((n_req,), jnp.int32),
+            pltpu.SMEM((n_req,), jnp.int32),
+            pltpu.VMEM((n_seq, 128), BF16),
+            pltpu.VMEM((n_seq, 128), BF16),
+            pltpu.VMEM((1, 128), F32),
+        ]
+        scratch += [pltpu.VMEM(w.shape, w.dtype) for w in weights]
         scratch += [
             pltpu.VMEM((n_req // 2, ctx, 128), BF16),
             pltpu.VMEM((n_seq, 128), F32),
@@ -629,7 +651,7 @@
             pltpu.VMEM((n_seq, r_own, 128), BF16),
             pltpu.VMEM((n_seq, r_own, 128), BF16),
             pltpu.VMEM((n_seq, r_own, 128), BF16),
-            pltpu.SemaphoreType.DMA((16,)),
+            pltpu.SemaphoreType.DMA((21,)),
             pltpu.SemaphoreType.DMA((10,)),
             pltpu.SemaphoreType.DMA((3, n_own)),
             pltpu.SemaphoreType.DMA((7, n_seq)),
@@ -637,7 +659,7 @@
         return pl.pallas_call(
             functools.partial(layer_kernel, n_tok, n_seq, n_kv),
             out_shape=jax.ShapeDtypeStruct((n_req // n_own, steps, 128), BF16),
-            in_specs=[smem, smem, smem, vmem, vmem, vmem] + [hbm] * len(weights),
+            in_specs=[hbm] * (6 + len(weights)),
             out_specs=vmem,
             scratch_shapes=scratch,
             compiler_params=pltpu.CompilerParams(

time: 57.8 us -> 55.8 us (0.965)
  Pallas kernels: 56.3 us -> 54.3 us
    pallas_call x1, Pallas kernels: 56.3 us -> 54.3 us  [per_device(): pl.pallas_call(functools.partial(layer_kernel, n_tok, n_seq, n_kv), out_s...]
where the time goes in v4:
time: 55.8 us; the launch traced here: 55.6 us
  Pallas kernels  54.3 us (97%)
  local copies, waits for them, and re-layouts  1.3 us (2%)
    pallas_call x1, Pallas kernels, per_device(): pl.pallas_call(functools.partial(layer_kernel, n_tok, n_seq, n_kv), out_s...  54.3 us
    unnamed x1, local copies, waits for them, and re-layouts  1.3 us

profile of v4, /device:TPU:0, one launch (start us, length us, event | category | flops | bytes accessed | tf_op | source)
XLA Modules:
  0.0 55.6 jit_solution(15742952643331691847)
XLA Ops:
  0.0 54.3 %layer.1 = bf16[8,4,128]{2,1,0:T(4,128)(2,1)} custom-call(s32[4,64]{1,0:T(4,128)} %bitcast.9, s32[64]{0:T(128)} %order_hbm.1, s32[64]{0:T(128)} %len_hbm.1, bf16[16,128]{1,0:T(8,128)(2,1)} %bitcast.7, bf16[16,128]{1,0:T(8,128)(2,1)} %bitcast.8, f32[1,128]{1,0:T(1,128)} %constant.2.clone.freq_hbm, bf16[4096,128]{1,0:T(8,128)(2,1)} %table_hbm.1, ...), custom_call_target="tpu_custom_call" | custom-call | tf_op jit(solution)/shard_map/layer/pallas_call | solution.py:659
  54.3 1.3 %copy.16 = bf16[8,4,128]{2,1,0:T(4,128)(2,1)} copy(bf16[8,4,128]{2,1,0:T(4,128)(2,1)} %layer.1) | data formatting | bytes 16384

commit v5 on v4

--- a/solution.py
+++ b/solution.py
@@ -84,7 +84,6 @@
     st_send,
     st_recv,
     st_t,
-    at_all,
     o_send,
     o_recv,
     mid_all,
@@ -127,6 +126,7 @@
 
     table_load = load(table_hbm, table)
     small_loads = [load(ids_hbm, ids_ref), load(order_hbm, order_ref), load(len_hbm, len_ref)]
+    wo_load = load(wo_hbm, wo.at[seq])
     barrier = pltpu.get_barrier_semaphore()
     for d in range(1, n_own):
         pl.semaphore_signal(
@@ -144,7 +144,6 @@
         load(cache_hbm.at[pl.ds(c, chunk)], cache.at[pl.ds(c, chunk)])
         for c in range(0, n_req, chunk)
     ]
-    wo_load = load(wo_hbm, wo)
     wg_load = load(wg_hbm, wg)
     wu_load = load(wu_hbm, wu)
     wd_load = load(wd_hbm, wd)
@@ -226,6 +225,18 @@
 
     for g in owners:
         own_copy(0, x_send.at[g], x_recv.at[own], g).start()
+
+    def share_wo(k):
+        for a in range(2):
+            s = pair_at(k) * 2 + a
+
+            @pl.when(s != seq)
+            def _():
+                seq_copy(7, wo.at[seq], wo.at[seq], s).start()
+
+    wo_load.wait()
+    share_wo(jnp.int32(2))
+    share_wo(jnp.int32(5))
     x_recv[own] = x_send[own]
     own_wait(0, x_recv)
     x_own = x_recv[0].astype(F32)
@@ -428,10 +439,12 @@
 
     def attend(i, carry):
         arrive(2 * i + 1)
+        share_wo(4 + i + (i + 1) // 2)
         following = score(2 * i + 1, s_odd)
         weigh(2 * i, s_even, p_even, *carry)
         deliver(2 * i)
         arrive(2 * i + 2)
+        share_wo(i + i // 2)
         carry = score(2 * i + 2, s_even)
         weigh(2 * i + 1, s_odd, p_odd, *following)
         deliver(2 * i + 1)
@@ -477,28 +490,53 @@
         )
         for t in range(2)
     ]
-    at_all[seq] = jnp.concatenate(at_rows, axis=1).astype(BF16)
-    for k in far:
-        for a in range(2):
-            s = near[k] * 2 + a
-            if k:
-                seq_copy(4, at_all.at[seq], at_all.at[seq], s).start()
-            else:
-
-                @pl.when(s != seq)
-                def _():
-                    seq_copy(4, at_all.at[seq], at_all.at[seq], s).start()
-    wo_load.wait()
-    seq_wait_all(4, at_all)
-    partial = dot(at_all[...].reshape(n_rows, 256), wo[...]).astype(BF16)
-    o_send[...] = partial.reshape(n_own, rows_own, 128)
-    for g in owners:
-        own_copy(2, o_send.at[g], o_recv.at[own], g).start()
-    o_recv[own] = o_send[own]
-    own_wait(2, o_recv)
-    attn = o_recv[0].astype(F32)
-    for g in range(1, n_own):
-        attn = attn + o_recv[g].astype(F32)
+    at = jnp.concatenate(at_rows, axis=1).astype(BF16)
+    holder = seq // halves
+    slot = own * halves + lax.rem(seq, halves)
+
+    def o_copy(s):
+        return pltpu.make_async_remote_copy(
+            src_ref=o_send.at[s],
+            dst_ref=o_recv.at[slot],
+            send_sem=send_sem.at[7],
+            recv_sem=seq_sem.at[4, slot],
+            device_id=(holder // n_kv, s, lax.rem(holder, n_kv)),
+            device_id_type=MESH,
+        )
+
+    seq_wait_all(7, wo)
+    for ks in (far[:4], far[4:]):
+        columns = [wo[near[k] * 2 + a] for k in ks for a in range(2)]
+        partial = dot(at, jnp.concatenate(columns, axis=1)).astype(BF16)
+        for n, k in enumerate(ks):
+            for a in range(2):
+                s = near[k] * 2 + a
+                o_send[s] = partial[:, n * 256 + a * 128 : n * 256 + (a + 1) * 128]
+                if k:
+                    o_copy(s).start()
+                else:
+
+                    @pl.when(jnp.logical_not(holds_own) | (s != seq))
+                    def _():
+                        o_copy(s).start()
+
+    @pl.when(holds_own)
+    def _():
+        o_recv[seq] = o_send[seq]
+
+    for s in range(n_seq):
+
+        @pl.when(jnp.logical_not(holds_own) | (seq != s))
+        def _():
+            seq_wait(4, o_recv, s)
+
+    attn_rows = []
+    for half in range(halves):
+        total = o_recv[half].astype(F32)
+        for g in range(1, n_own):
+            total = total + o_recv[g * halves + half].astype(F32)
+        attn_rows.append(total)
+    attn = jnp.concatenate(attn_rows, axis=0)
     mid = (x_own + attn).astype(BF16)
     mid_all[seq] = mid
     for k in far:
@@ -565,19 +603,20 @@
     out_ref[...] = result.astype(BF16).reshape(out_ref.shape)
 
     sent(0, x_recv, n_own - 1)
-    sent(2, o_recv, n_own - 1)
     sent(3, x_rows, n_seq - 1)
 
     @pl.when(jnp.logical_not(holds_own))
     def _():
         sent(3, x_rows, 1)
+        sent(7, o_recv, 1)
 
     sent(4, q_all, n_seq - 1)
     sent(5, acc_recv, n_seq - 1)
     sent(6, st_recv, n_seq - 1)
-    sent(7, at_all, n_seq - 1)
+    sent(7, o_recv, n_seq - 1)
     sent(8, mid_all, n_seq - 1)
     sent(9, d_recv, n_seq - 1)
+    sent(10, wo, n_seq - 1)
 
 
 def solution(mesh):
@@ -626,7 +665,9 @@
             pltpu.VMEM((n_seq, 128), BF16),
             pltpu.VMEM((1, 128), F32),
         ]
-        scratch += [pltpu.VMEM(w.shape, w.dtype) for w in weights]
+        held = [w.shape for w in weights]
+        held[4] = (n_seq, *proj_out.shape)
+        scratch += [pltpu.VMEM(shape, BF16) for shape in held]
         scratch += [
             pltpu.VMEM((n_req // 2, ctx, 128), BF16),
             pltpu.VMEM((n_seq, 128), F32),
@@ -645,16 +686,15 @@
             pltpu.VMEM((n_req // 8, 2, 128), F32),
             pltpu.VMEM((n_seq, 2, 128), F32),
             pltpu.VMEM((128, 128), F32),
-            pltpu.VMEM((n_seq, r_seq, 256), BF16),
-            pltpu.VMEM((n_own, r_own, 128), BF16),
-            pltpu.VMEM((n_own, r_own, 128), BF16),
+            pltpu.VMEM((n_seq, r_seq, 128), BF16),
+            pltpu.VMEM((n_seq, r_seq, 128), BF16),
             pltpu.VMEM((n_seq, r_own, 128), BF16),
             pltpu.VMEM((n_seq, r_own, 128), BF16),
             pltpu.VMEM((n_seq, r_own, 128), BF16),
             pltpu.SemaphoreType.DMA((21,)),
-            pltpu.SemaphoreType.DMA((10,)),
-            pltpu.SemaphoreType.DMA((3, n_own)),
-            pltpu.SemaphoreType.DMA((7, n_seq)),
+            pltpu.SemaphoreType.DMA((11,)),
+            pltpu.SemaphoreType.DMA((1, n_own)),
+            pltpu.SemaphoreType.DMA((8, n_seq)),
         ]
         return pl.pallas_call(
             functools.partial(layer_kernel, n_tok, n_seq, n_kv),

time: 55.8 us -> 54.7 us (0.980)
  Pallas kernels: 54.3 us -> 53.2 us
    pallas_call x1, Pallas kernels: 54.3 us -> 53.2 us  [per_device(): pl.pallas_call(functools.partial(layer_kernel, n_tok, n_seq, n_kv), out_s...]
where the time goes in v5:
time: 54.7 us; the launch traced here: 54.5 us
  Pallas kernels  53.2 us (97%)
  local copies, waits for them, and re-layouts  1.3 us (2%)
    pallas_call x1, Pallas kernels, per_device(): pl.pallas_call(functools.partial(layer_kernel, n_tok, n_seq, n_kv), out_s...  53.2 us
    unnamed x1, local copies, waits for them, and re-layouts  1.3 us

profile of v5, /device:TPU:0, one launch (start us, length us, event | category | flops | bytes accessed | tf_op | source)
XLA Modules:
  0.0 54.5 jit_solution(2049307786846974739)
XLA Ops:
  0.0 53.2 %layer.1 = bf16[8,4,128]{2,1,0:T(4,128)(2,1)} custom-call(s32[4,64]{1,0:T(4,128)} %bitcast.9, s32[64]{0:T(128)} %order_hbm.1, s32[64]{0:T(128)} %len_hbm.1, bf16[16,128]{1,0:T(8,128)(2,1)} %bitcast.7, bf16[16,128]{1,0:T(8,128)(2,1)} %bitcast.8, f32[1,128]{1,0:T(1,128)} %constant.2.clone.freq_hbm, bf16[4096,128]{1,0:T(8,128)(2,1)} %table_hbm.1, ...), custom_call_target="tpu_custom_call" | custom-call | tf_op jit(solution)/shard_map/layer/pallas_call | solution.py:699
  53.2 1.3 %copy.16 = bf16[8,4,128]{2,1,0:T(4,128)(2,1)} copy(bf16[8,4,128]{2,1,0:T(4,128)(2,1)} %layer.1) | data formatting | bytes 16384
